TPU v7x, 768 devices: a whole 4x8x12 slice. The times are simulated.
768 devices in a mesh: row: 8 (over y_hi, x), col: 96 (over z, y_lo, core).
Axes of the slice: x: 4, y: 8 (y_hi: 2, y_lo: 4; y = y_hi * 4 + y_lo), z: 12, core: 2. Of those that a mesh axis runs over, the one named last changes fastest.
Arguments:
- tokens: bfloat16 [384, 8192], P('col', 'row'), may hold values from -6 to 6
- out_grad: bfloat16 [384, 8192], P('col', 'row'), may hold values from -6 to 6
- gate_weight: bfloat16 [8192, 27648], P('row', 'col'), may hold values from -0.0625 to 0.0625
- up_weight: bfloat16 [8192, 27648], P('row', 'col'), may hold values from -0.0625 to 0.0625
- down_weight: bfloat16 [27648, 8192], P('col', 'row'), may hold values from -0.0390625 to 0.0390625
Outputs:
- tokens_grad: bfloat16 [384, 8192], P('col', 'row')
- gate_grad: bfloat16 [8192, 27648], P('row', 'col')
- up_grad: bfloat16 [8192, 27648], P('row', 'col')
- down_grad: bfloat16 [27648, 8192], P('col', 'row')
All inputs are finite; a program needn't handle non-finite values.
Results may differ from a plain program's by a relative error of at most 0.0049.
Values may be sent and summed in bfloat16 or wider, within the bound.
No kernel may reach another device: no remote copies, remote signals or barrier semaphores. Data moves between devices by JAX's collectives and lax.ppermute only.
A program may use at most 32 MiB of HBM per device.

v0:
```python
import jax
import jax.numpy as jnp
from jax import lax
from jax.sharding import PartitionSpec as P


def contract_last(left, right):
    return lax.dot_general(
        left, right, (((1,), (1,)), ((), ())), preferred_element_type=jnp.float32
    )


def contract_first(left, right):
    return lax.dot_general(
        left, right, (((0,), (0,)), ((), ())), preferred_element_type=jnp.float32
    )


def pointwise(gate_pre, up_pre, hidden_grad):
    sig = jax.nn.sigmoid(gate_pre)
    act = gate_pre * sig
    hidden = (act * up_pre).astype(jnp.bfloat16)
    up_delta = (hidden_grad * act).astype(jnp.bfloat16)
    gate_delta = (hidden_grad * up_pre * sig * (1.0 + gate_pre * (1.0 - sig))).astype(jnp.bfloat16)
    return (hidden, gate_delta, up_delta)


def per_device(tokens, out_grad, gate_weight, up_weight, down_weight):
    panel_in, panel_grad = (
        lax.all_gather(tokens, "col", axis=0, tiled=True),
        lax.all_gather(out_grad, "col", axis=0, tiled=True),
    )
    factor = float(panel_in.shape[0]) ** (-0.5)
    gate_part = jnp.dot(panel_in, gate_weight, preferred_element_type=jnp.float32)
    up_part = jnp.dot(panel_in, up_weight, preferred_element_type=jnp.float32)
    grad_part = contract_last(panel_grad, down_weight)
    gate_pre, up_pre, hidden_grad = lax.psum((gate_part, up_part, grad_part), "row")
    hidden, gate_delta, up_delta = pointwise(gate_pre, up_pre, hidden_grad)
    down_grad = (contract_first(hidden, panel_grad) * factor).astype(jnp.bfloat16)
    gate_grad = (contract_first(panel_in, gate_delta) * factor).astype(jnp.bfloat16)
    up_grad = (contract_first(panel_in, up_delta) * factor).astype(jnp.bfloat16)
    tokens_grad = lax.psum_scatter(
        contract_last(gate_delta, gate_weight) + contract_last(up_delta, up_weight),
        "col",
        scatter_dimension=0,
        tiled=True,
    ).astype(jnp.bfloat16)
    return (tokens_grad, gate_grad, up_grad, down_grad)


def solution(mesh):
    return jax.shard_map(
        per_device,
        mesh=mesh,
        in_specs=(
            P("col", "row"),
            P("col", "row"),
            P("row", "col"),
            P("row", "col"),
            P("col", "row"),
        ),
        out_specs=(P("col", "row"), P("row", "col"), P("row", "col"), P("col", "row")),
        check_vma=False,
    )
```

profile of v0, /device:TPU:6, one launch (start us, length us, event | category | flops | bytes accessed | tf_op | source)
XLA Modules:
  0.0 797.4 jit_solution(6691259630697225421)
XLA Ops:
  7.2 0.0 copy-start
  7.2 0.0 all-reduce.5.cloned.1.call-start
  7.2 127.9 %all-gather.1 = bf16[96,4,1024]{2,1,0:T(4,128)(2,1)S(1)} all-gather(bf16[1,4,1024]{2,1,0:T(4,128)(2,1)} %bitcast.22), channel_id=1, replica_groups=mesh['row'=8,'col'=96] {'col'}, dimensions={0}, use_global_device_ids=true | all-gather | bytes 794624 | tf_op jit(solution)/shard_map/all_gather | solution.py:30
  135.1 0.2 reshape.11
  135.3 0.0 copy-done
  135.3 0.0 copy-start.1
  135.3 1.3 fusion.10
  136.6 0.0 copy-done.1
  136.6 0.0 copy-start.5
  136.6 1.3 fusion.9
  137.9 0.0 copy-done.5
  137.9 112.1 %all-gather = bf16[96,4,1024]{2,1,0:T(4,128)(2,1)S(1)} all-gather(bf16[1,4,1024]{2,1,0:T(4,128)(2,1)S(1)} %bitcast.23), channel_id=1, replica_groups=mesh['row'=8,'col'=96] {'col'}, dimensions={0}, use_global_device_ids=true | all-gather | bytes 794624 | tf_op jit(solution)/shard_map/all_gather | solution.py:31
  249.9 0.2 reshape.9
  250.1 2.3 fusion.8
  252.5 0.0 all-reduce.5.cloned.1.call-update
  252.5 1.3 dynamic-slice
  254.4 118.8 %all-reduce.5.cloned.1.call-done = (f32[384,288]{0,1:T(8,128)}, f32[384,288]{0,1:T(8,128)}, f32[384,288]{0,1:T(8,128)}) async-done(((f32[384,288]{0,1:T(8,128)}, f32[384,288]{0,1:T(8,128)}, f32[384,288]{0,1:T(8,128)}), (f32[384,288]{0,1:T(8,128)}, f32[384,288]{0,1:T(8,128)}, f32[384,288]{0,1:T(8,128)})) %all-reduce.5.cloned.1.call-update) | async-done | bytes 1327120 | tf_op jit(solution)/shard_map/psum | solution.py:37
  373.3 0.0 copy-start.2
  373.3 0.0 copy-start.3
  373.3 0.0 copy-start.4
  373.3 2.6 fusion.2
  375.8 0.0 copy-done.2
  375.8 0.0 copy-done.3
  375.8 0.0 copy-done.4
  375.8 0.3 multiply_convert_fusion.1
  376.1 1.3 fusion.4
  377.4 0.6 fusion.11
  378.0 1.3 fusion.3
  379.3 0.6 convolution_add_fusion
  379.9 410.1 %all-reduce.6 = bf16[384,1024]{1,0:T(8,128)(2,1)S(1)} all-reduce(f32[384,1024]{1,0:T(8,128)S(1)} %convolution_add_fusion), channel_id=2, replica_groups=mesh['row'=8,'col'=96] {'col'}, use_global_device_ids=true, to_apply=%region_3.0.clone | all-reduce | flops 393216 | bytes 2359296
  790.0 0.6 dynamic-slice_convert_fusion
Async XLA Ops:
  7.2 128.1 %copy-start = (bf16[1024,288]{0,1:T(8,128)(2,1)S(1)}, bf16[1024,288]{0,1:T(8,128)(2,1)}, u32[]{:S(2)}) copy-start(bf16[1024,288]{0,1:T(8,128)(2,1)} %param.7) | copy-start | bytes 1769476
  7.2 366.1 %all-reduce.5.cloned.1.call-start = ((), (), s32[]{:S(2)}) async-start(), calls=%async_computation | async-start | bytes 2654208 | tf_op jit(solution)/shard_map/psum | solution.py:37
  135.3 1.3 copy-start.1
  136.6 1.3 copy-start.5
  373.3 2.6 copy-start.2
  373.3 2.6 copy-start.3
  373.3 2.6 copy-start.4
Sparse Core Ops, SparseCore 0:
  252.6 120.6 all-reduce.4
where the time goes:
time: 798 us; the launch traced here: 797 us
  blocking collectives  650 us (81%)
  waiting for transfers between devices  119 us (15%)
  between operations  14.8 us (2%)
  matrix products  11.2 us (1%)
    unnamed x1, blocking collectives  410 us
    all_gather x1, blocking collectives, per_device(): lax.all_gather(tokens, 'col', axis=0, tiled=True)  128 us
    psum x1, waiting for transfers between devices, per_device(): lax.psum((gate_part, up_part, grad_part), 'row')  119 us
    all_gather x1, blocking collectives, per_device(): lax.all_gather(out_grad, 'col', axis=0, tiled=True)  112 us
  transfers between devices with their start and end apart: 1, of which 1 were waited for; matrix products, arithmetic and copies ran while one was open for 0% of the time, Pallas kernels for 0%

commit v1 on v0

v1 whole, which is shorter than its diff:
```python
import jax
import jax.numpy as jnp
import numpy as np
from jax import lax
from jax.sharding import Mesh, PartitionSpec as P

F32 = jnp.float32
BF16 = jnp.bfloat16
SWAP = [(0, 1), (1, 0)]
ROW = ("yh", "x")
CHIPS = ("z", "yl")


def dot(left, right, left_dim, right_dim):
    return lax.dot_general(
        left, right, (((left_dim,), (right_dim,)), ((), ())), preferred_element_type=F32
    )


def pointwise(gate_pre, up_pre, hidden_grad):
    sig = jax.nn.sigmoid(gate_pre)
    act = gate_pre * sig
    hidden = (act * up_pre).astype(BF16)
    up_delta = (hidden_grad * act).astype(BF16)
    gate_delta = (hidden_grad * up_pre * sig * (1.0 + gate_pre * (1.0 - sig))).astype(BF16)
    return hidden, gate_delta, up_delta


def exchange_sum(parts, axes):
    me = lax.axis_index(axes)
    own = lax.dynamic_index_in_dim(parts, me, 0)
    got = lax.all_to_all(parts.astype(BF16), axes, 0, 0).astype(F32)
    at = lax.broadcasted_iota(jnp.int32, got.shape, 0)
    return jnp.sum(jnp.where(at == me, own, got), axis=0)


def gather(block, axes):
    copies = jnp.broadcast_to(block[None], (lax.axis_size(axes),) + block.shape)
    return lax.all_to_all(copies, axes, 0, 0)


def per_device(tokens, out_grad, gate_weight, up_weight, down_weight):
    rows, width = tokens.shape
    units = gate_weight.shape[1]
    n_row = lax.axis_size(ROW)
    mine = gather(jnp.concatenate([tokens, out_grad], 1), CHIPS)
    mine = mine.reshape(-1, 2 * width)
    panel = jnp.concatenate([mine, lax.ppermute(mine, "core", SWAP)])
    panel_in, panel_grad = panel[:, :width], panel[:, width:]
    count = panel.shape[0]
    factor = float(count) ** (-0.5)

    share = units // n_row
    pre = jnp.concatenate(
        [
            dot(gate_weight, panel_in, 0, 1).reshape(n_row, share, count),
            dot(up_weight, panel_in, 0, 1).reshape(n_row, share, count),
            dot(down_weight, panel_grad, 1, 1).reshape(n_row, share, count),
        ],
        axis=1,
    )
    total = exchange_sum(pre, ROW)
    deltas = pointwise(total[:share], total[share : 2 * share], total[2 * share :])
    deltas = gather(jnp.concatenate(deltas), ROW)
    hidden = deltas[:, :share].reshape(units, count)
    gate_delta = deltas[:, share : 2 * share].reshape(units, count)
    up_delta = deltas[:, 2 * share :].reshape(units, count)

    partial = dot(gate_delta, gate_weight, 0, 1) + dot(up_delta, up_weight, 0, 1)
    half = count // 2
    acc = partial[:half] + lax.ppermute(partial[half:], "core", SWAP)
    tokens_grad = exchange_sum(acc.reshape(-1, rows, width), CHIPS).astype(BF16)

    down_grad = (dot(hidden, panel_grad, 1, 0) * factor).astype(BF16)
    gate_grad = (dot(panel_in, gate_delta, 0, 1) * factor).astype(BF16)
    up_grad = (dot(panel_in, up_delta, 0, 1) * factor).astype(BF16)
    return tokens_grad, gate_grad, up_grad, down_grad


def solution(mesh):
    n_row, n_col = mesh.devices.shape
    grid = np.asarray(mesh.devices).reshape(2, n_row // 2, n_col // 8, 4, 2)
    fine = Mesh(grid, ("yh", "x", "z", "yl", "core"))
    row, col = ("yh", "x"), ("z", "yl", "core")
    return jax.shard_map(
        per_device,
        mesh=fine,
        in_specs=(P(col, row), P(col, row), P(row, col), P(row, col), P(col, row)),
        out_specs=(P(col, row), P(row, col), P(row, col), P(col, row)),
        check_vma=False,
    )
```

time: 798 us -> 153 us (0.19)
  blocking collectives: 650 us -> 72.9 us
  waiting for transfers between devices: 119 us -> 34.5 us
  starting transfers between devices: 0.04 us -> 24.7 us
  between operations: 14.8 us -> 0.89 us
    unnamed x1 -> x0, blocking collectives: 410 us -> none
    all_gather x2 -> x0, blocking collectives: 240 us -> none  [the longest x1 128 us: per_device(): lax.all_gather(tokens, 'col', axis=0, tiled=True)]
    psum x1 -> x0, waiting for transfers between devices: 119 us -> none  [per_device(): lax.psum((gate_part, up_part, grad_part), 'row')]
    all_to_all x0 -> x2, blocking collectives: none -> 72.9 us  [gather(): return lax.all_to_all(copies, axes, 0, 0)]
    all_to_all x0 -> x2, waiting for transfers between devices: none -> 30 us  [exchange_sum(): got = lax.all_to_all(parts.astype(BF16), axes, 0, 0).astype(F32)]
    all_to_all x0 -> x2, starting transfers between devices: none -> 20.7 us  [exchange_sum(): got = lax.all_to_all(parts.astype(BF16), axes, 0, 0).astype(F32)]
  transfers between devices with their start and end apart: 1 -> 4, of which waited for: 1 -> 4; matrix products, arithmetic and copies ran while one was open for 0% -> 3% of each run, Pallas kernels for 0% -> 0%
where the time goes in v1:
time: 153 us; the launch traced here: 150 us
  blocking collectives  72.9 us (48%)
  waiting for transfers between devices  34.5 us (23%)
  starting transfers between devices  24.7 us (16%)
  matrix products  10 us (7%)
  other arithmetic  3.97 us (3%)
  local copies, waits for them, and re-layouts  3.41 us (2%)
    all_to_all x2, blocking collectives, gather(): return lax.all_to_all(copies, axes, 0, 0)  72.9 us
    all_to_all x2, waiting for transfers between devices, exchange_sum(): got = lax.all_to_all(parts.astype(BF16), axes, 0, 0).astype(F32)  30 us
    all_to_all x2, starting transfers between devices, exchange_sum(): got = lax.all_to_all(parts.astype(BF16), axes, 0, 0).astype(F32)  20.7 us
    dot_general x8, matrix products, dot(): lax.dot_general(left, right, (((left_dim,), (right_dim,)), ((), ())), pre...  10 us
  transfers between devices with their start and end apart: 4, of which 4 were waited for; matrix products, arithmetic and copies ran while one was open for 3% of the time, Pallas kernels for 0%

profile of v1, /device:TPU:6, one launch (start us, length us, event | category | flops | bytes accessed | tf_op | source)
XLA Modules:
  0.0 150.3 jit_solution(15309352214023582652)
XLA Ops:
  0.6 0.0 copy-start
  0.6 0.8 pad_maximum_fusion.2
  1.4 0.4 broadcast_in_dim.32
  1.8 51.9 %all_to_all.20 = bf16[48,4,2048]{2,1,0:T(4,128)(2,1)S(1)} all-to-all(bf16[48,4,2048]{2,1,0:T(4,128)(2,1)S(1)} %broadcast_in_dim.32), channel_id=1, replica_groups=mesh['yh'=2,'x'=4,'z'=12,'yl'=4,'core'=2] {'z','yl'}, dimensions={0} | all-to-all | bytes 1572864 | tf_op jit(solution)/shard_map/all_to_all | solution.py:39
  53.7 0.2 reshape.34
  53.9 0.0 copy-start.1
  53.9 2.1 %collective-permute-start = (bf16[192,2048]{1,0:T(8,128)(2,1)S(1)}, bf16[192,2048]{1,0:T(8,128)(2,1)S(1)}, u32[]{:S(2)}, u32[]{:S(2)}) collective-permute-start(bf16[192,2048]{1,0:T(8,128)(2,1)S(1)} %reshape.34), channel_id=1, source_target_pairs={{0,1},{1,0},{2,3},{3,2},{4,5},{5,4},{6,7},{7,6},{8,9},{9,8},{10,11... | collective-permute-start | bytes 2359304 | tf_op jit(solution)/shard_map/ppermute | solution.py:48
  56.0 0.1 constant_dynamic-update-slice_fusion.1
  56.0 2.2 %collective-permute-done = bf16[192,2048]{1,0:T(8,128)(2,1)S(1)} collective-permute-done((bf16[192,2048]{1,0:T(8,128)(2,1)S(1)}, bf16[192,2048]{1,0:T(8,128)(2,1)S(1)}, u32[]{:S(2)}, u32[]{:S(2)}) %collective-permute-start) | collective-permute-done | bytes 786464 | tf_op jit(solution)/shard_map/ppermute | solution.py:48
  58.2 0.1 constant_dynamic-update-slice_fusion
  58.3 0.0 copy-start.3
  58.3 1.1 copy-done.3
  59.4 0.0 copy-done.1
  59.4 0.0 copy-start.5
  59.4 0.5 convolution_bitcast_fusion.1
  60.0 0.5 copy-done.5
  60.5 1.6 %convolution_bitcast_fusion = f32[288,384]{1,0:T(8,128)S(1)} fusion(bf16[288,1024]{1,0:T(8,128)(2,1)S(1)} %copy-done.5, bf16[384,2048]{1,0:T(8,128)(2,1)} %copy-done.3), kind=kOutput, calls=%fused_computation.9 | convolution fusion | flops 226492416 | bytes 1818624 | tf_op jit(solution)/shard_map/dot_general | solution.py:15
  62.2 0.0 copy-done
  62.2 1.6 %convolution_bitcast_fusion.2 = f32[288,384]{1,0:T(8,128)S(1)} fusion(bf16[1024,288]{0,1:T(8,128)(2,1)S(1)} %copy-done, bf16[384,2048]{1,0:T(8,128)(2,1)} %copy-done.3), kind=kOutput, calls=%fused_computation.11 | convolution fusion | flops 226492416 | bytes 1818624 | tf_op jit(solution)/shard_map/dot_general | solution.py:15
  63.9 1.0 fusion.10
  64.9 7.3 %all-to-all-start.1 = ((bf16[8,108,384]{2,1,0:T(8,128)(2,1)}), bf16[8,108,384]{2,1,0:T(8,128)(2,1)S(1)}, u32[]{:S(2)}, u32[]{:S(2)}) async-start(bf16[8,108,384]{2,1,0:T(8,128)(2,1)} %get-tuple-element.4), calls=%async_computation.1 | async-start | bytes 1376256 | tf_op jit(solution)/shard_map/all_to_all | solution.py:32
  72.3 13.8 %all-to-all-done.1 = bf16[8,108,384]{2,1,0:T(8,128)(2,1)S(1)} async-done(((bf16[8,108,384]{2,1,0:T(8,128)(2,1)}), bf16[8,108,384]{2,1,0:T(8,128)(2,1)S(1)}, u32[]{:S(2)}, u32[]{:S(2)}) %all-to-all-start.1) | async-done | bytes 663584 | tf_op jit(solution)/shard_map/all_to_all | solution.py:32
  86.1 0.2 select_reduce_fusion
  86.4 0.1 broadcast_in_dim.35
  86.4 21.0 %all_to_all.21 = bf16[8,108,384]{2,1,0:T(8,128)(2,1)S(1)} all-to-all(bf16[8,108,384]{2,1,0:T(8,128)(2,1)S(1)} %broadcast_in_dim.35), channel_id=1, replica_groups=mesh['yh'=2,'x'=4,'z'=12,'yl'=4,'core'=2] {'yh','x'}, dimensions={0} | all-to-all | bytes 1327104 | tf_op jit(solution)/shard_map/all_to_all | solution.py:39
  107.4 0.1 fusion.11
  107.5 0.0 copy-start.2
  107.6 0.6 fusion.12
  108.2 0.3 copy-done.2
  108.6 0.6 convolution_add_fusion
  109.2 0.1 slice.48
  109.2 1.9 %collective-permute-start.1 = (f32[192,1024]{1,0:T(8,128)S(1)}, f32[192,1024]{1,0:T(8,128)S(1)}, u32[]{:S(2)}, u32[]{:S(2)}) collective-permute-start(f32[192,1024]{1,0:T(8,128)S(1)} %slice.48), channel_id=1, source_target_pairs={{0,1},{1,0},{2,3},{3,2},{4,5},{5,4},{6,7},{7,6},{8,9},{9,8},{10,11... | collective-permute-start | bytes 2359304 | tf_op jit(solution)/shard_map/ppermute | solution.py:71
  111.2 2.3 %collective-permute-done.1 = f32[192,1024]{1,0:T(8,128)S(1)} collective-permute-done((f32[192,1024]{1,0:T(8,128)S(1)}, f32[192,1024]{1,0:T(8,128)S(1)}, u32[]{:S(2)}, u32[]{:S(2)}) %collective-permute-start.1) | collective-permute-done | bytes 786464 | tf_op jit(solution)/shard_map/ppermute | solution.py:71
  113.4 0.1 slice_add_fusion
  113.5 0.2 reshape.40
  113.7 0.9 convert_element_type.38
  114.6 13.4 %all-to-all-start.3 = ((bf16[48,4,1024]{2,1,0:T(4,128)(2,1)}), bf16[48,4,1024]{2,1,0:T(4,128)(2,1)S(1)}, u32[]{:S(2)}, u32[]{:S(2)}) async-start(bf16[48,4,1024]{2,1,0:T(4,128)(2,1)} %convert_element_type.38), calls=%async_computation.3 | async-start | bytes 786432 | tf_op jit(solution)/shard_map/all_to_all | solution.py:32
  128.1 0.0 copy-start.4
  128.1 2.5 %fusion.1 = bf16[1024,288]{0,1:T(8,128)(2,1)} fusion(bf16[288,384]{1,0:T(8,128)(2,1)S(1)} %reshape.38, bf16[384,2048]{1,0:T(8,128)(2,1)} %copy-done.3), kind=kOutput, calls=%fused_computation.7 | convolution fusion | flops 227082240 | bytes 1597440 | tf_op jit(solution)/shard_map/dot_general | solution.py:15
  130.6 0.0 copy-done.4
  130.6 1.3 fusion.2
  131.9 1.3 fusion
  133.2 16.2 %all-to-all-done.3 = bf16[48,4,1024]{2,1,0:T(4,128)(2,1)S(1)} async-done(((bf16[48,4,1024]{2,1,0:T(4,128)(2,1)}), bf16[48,4,1024]{2,1,0:T(4,128)(2,1)S(1)}, u32[]{:S(2)}, u32[]{:S(2)}) %all-to-all-start.3) | async-done | bytes 393248 | tf_op jit(solution)/shard_map/all_to_all | solution.py:32
  149.5 0.9 select_reduce_fusion.1
  (12 shorter events, 0.4 us)
Async XLA Ops:
  0.6 61.6 %copy-start = (bf16[1024,288]{0,1:T(8,128)(2,1)S(1)}, bf16[1024,288]{0,1:T(8,128)(2,1)}, u32[]{:S(2)}) copy-start(bf16[1024,288]{0,1:T(8,128)(2,1)} %param.7) | copy-start | bytes 1769476
  53.9 5.6 %copy-start.1 = (bf16[1024,288]{0,1:T(8,128)(2,1)S(1)}, bf16[1024,288]{0,1:T(8,128)(2,1)}, u32[]{:S(2)}) copy-start(bf16[1024,288]{0,1:T(8,128)(2,1)} %param.8) | copy-start | bytes 1769476
  53.9 4.3 %collective-permute-start = (bf16[192,2048]{1,0:T(8,128)(2,1)S(1)}, bf16[192,2048]{1,0:T(8,128)(2,1)S(1)}, u32[]{:S(2)}, u32[]{:S(2)}) collective-permute-start(bf16[192,2048]{1,0:T(8,128)(2,1)S(1)} %reshape.34), channel_id=1, source_target_pairs={{0,1},{1,0},{2,3},{3,2},{4,5},{5,4},{6,7},{7,6},{8,9},{9,8},{10,11... | collective-permute-start | bytes 2359304 | tf_op jit(solution)/shard_map/ppermute | solution.py:48
  58.3 1.1 copy-start.3
  59.4 1.1 copy-start.5
  64.9 21.2 %all-to-all-start.1 = ((bf16[8,108,384]{2,1,0:T(8,128)(2,1)}), bf16[8,108,384]{2,1,0:T(8,128)(2,1)S(1)}, u32[]{:S(2)}, u32[]{:S(2)}) async-start(bf16[8,108,384]{2,1,0:T(8,128)(2,1)} %get-tuple-element.4), calls=%async_computation.1 | async-start | bytes 1376256 | tf_op jit(solution)/shard_map/all_to_all | solution.py:32
  107.5 1.1 copy-start.2
  109.2 4.2 %collective-permute-start.1 = (f32[192,1024]{1,0:T(8,128)S(1)}, f32[192,1024]{1,0:T(8,128)S(1)}, u32[]{:S(2)}, u32[]{:S(2)}) collective-permute-start(f32[192,1024]{1,0:T(8,128)S(1)} %slice.48), channel_id=1, source_target_pairs={{0,1},{1,0},{2,3},{3,2},{4,5},{5,4},{6,7},{7,6},{8,9},{9,8},{10,11... | collective-permute-start | bytes 2359304 | tf_op jit(solution)/shard_map/ppermute | solution.py:71
  114.6 34.8 %all-to-all-start.3 = ((bf16[48,4,1024]{2,1,0:T(4,128)(2,1)}), bf16[48,4,1024]{2,1,0:T(4,128)(2,1)S(1)}, u32[]{:S(2)}, u32[]{:S(2)}) async-start(bf16[48,4,1024]{2,1,0:T(4,128)(2,1)} %convert_element_type.38), calls=%async_computation.3 | async-start | bytes 786432 | tf_op jit(solution)/shard_map/all_to_all | solution.py:32
  128.1 2.6 %copy-start.4 = (bf16[384,2048]{1,0:T(8,128)(2,1)S(1)}, bf16[384,2048]{1,0:T(8,128)(2,1)}, u32[]{:S(2)}) copy-start(bf16[384,2048]{1,0:T(8,128)(2,1)} %copy-done.3) | copy-start | bytes 4718596

commit v2 on v1

--- a/solution.py
+++ b/solution.py
@@ -7,8 +7,7 @@
 F32 = jnp.float32
 BF16 = jnp.bfloat16
 SWAP = [(0, 1), (1, 0)]
-ROW = ("yh", "x")
-CHIPS = ("z", "yl")
+CHIPS = ("yl", "z")
 
 
 def dot(left, right, left_dim, right_dim):
@@ -42,29 +41,30 @@
 def per_device(tokens, out_grad, gate_weight, up_weight, down_weight):
     rows, width = tokens.shape
     units = gate_weight.shape[1]
-    n_row = lax.axis_size(ROW)
-    mine = gather(jnp.concatenate([tokens, out_grad], 1), CHIPS)
+    n_x = lax.axis_size("x")
+    mine = lax.all_gather(jnp.concatenate([tokens, out_grad], 1), "z", axis=0)
+    mine = lax.all_gather(mine, "yl", axis=0)
     mine = mine.reshape(-1, 2 * width)
     panel = jnp.concatenate([mine, lax.ppermute(mine, "core", SWAP)])
     panel_in, panel_grad = panel[:, :width], panel[:, width:]
     count = panel.shape[0]
     factor = float(count) ** (-0.5)
 
-    share = units // n_row
-    pre = jnp.concatenate(
+    share = units // n_x
+    pre = jnp.stack(
         [
-            dot(gate_weight, panel_in, 0, 1).reshape(n_row, share, count),
-            dot(up_weight, panel_in, 0, 1).reshape(n_row, share, count),
-            dot(down_weight, panel_grad, 1, 1).reshape(n_row, share, count),
+            dot(gate_weight, panel_in, 0, 1).reshape(n_x, share, count),
+            dot(up_weight, panel_in, 0, 1).reshape(n_x, share, count),
+            dot(down_weight, panel_grad, 1, 1).reshape(n_x, share, count),
         ],
         axis=1,
     )
-    total = exchange_sum(pre, ROW)
-    deltas = pointwise(total[:share], total[share : 2 * share], total[2 * share :])
-    deltas = gather(jnp.concatenate(deltas), ROW)
-    hidden = deltas[:, :share].reshape(units, count)
-    gate_delta = deltas[:, share : 2 * share].reshape(units, count)
-    up_delta = deltas[:, 2 * share :].reshape(units, count)
+    part = exchange_sum(pre, "x")
+    total = part + lax.ppermute(part.astype(BF16), "yh", SWAP).astype(F32)
+    deltas = gather(jnp.stack(pointwise(total[0], total[1], total[2])), "x")
+    hidden = deltas[:, 0].reshape(units, count)
+    gate_delta = deltas[:, 1].reshape(units, count)
+    up_delta = deltas[:, 2].reshape(units, count)
 
     partial = dot(gate_delta, gate_weight, 0, 1) + dot(up_delta, up_weight, 0, 1)
     half = count // 2

time: 153 us -> 139 us (0.908)
  blocking collectives: 72.9 us -> 62.1 us
  local copies, waits for them, and re-layouts: 3.41 us -> 0.91 us
  matrix products: 10 us -> 7.77 us
    all_to_all x2 -> x1, blocking collectives: 72.9 us -> 11.2 us  [gather(): return lax.all_to_all(copies, axes, 0, 0)]
    all_gather x0 -> x2, blocking collectives: none -> 50.8 us  [the longest x1 33.3 us: per_device(): mine = lax.all_gather(jnp.concatenate([tokens, out_grad], 1), 'z', axis=0)]
    ppermute x0 -> x1, starting transfers between devices: none -> 7.23 us  [per_device(): total = part + lax.ppermute(part.astype(BF16), 'yh', SWAP).astype(F32)]
    all_to_all x2, starting transfers between devices: 20.7 us -> 14.8 us  [exchange_sum(): got = lax.all_to_all(parts.astype(BF16), axes, 0, 0).astype(F32)]
    ppermute x0 -> x1, waiting for transfers between devices: none -> 5.69 us  [per_device(): total = part + lax.ppermute(part.astype(BF16), 'yh', SWAP).astype(F32)]
    all_to_all x2, waiting for transfers between devices: 30 us -> 25.6 us  [exchange_sum(): got = lax.all_to_all(parts.astype(BF16), axes, 0, 0).astype(F32)]
    dot_general x8, matrix products: 10 us -> 7.77 us  [dot(): lax.dot_general(left, right, (((left_dim,), (right_dim,)), ((), ())), pre...]
    unnamed x13 -> x11, local copies, waits for them, and re-layouts: 2.08 us -> 0.23 us
  transfers between devices with their start and end apart: 4 -> 5, of which waited for: 4 -> 5; matrix products, arithmetic and copies ran while one was open for 3% -> 4% of each run, Pallas kernels for 0% -> 0%
where the time goes in v2:
time: 139 us; the launch traced here: 138 us
  blocking collectives  62.1 us (45%)
  waiting for transfers between devices  35.8 us (26%)
  starting transfers between devices  26 us (19%)
  matrix products  7.77 us (6%)
  other arithmetic  4.16 us (3%)
    all_gather x1, blocking collectives, per_device(): mine = lax.all_gather(jnp.concatenate([tokens, out_grad], 1), 'z', axis=0)  33.3 us
    all_to_all x2, waiting for transfers between devices, exchange_sum(): got = lax.all_to_all(parts.astype(BF16), axes, 0, 0).astype(F32)  25.6 us
    all_gather x1, blocking collectives, per_device(): mine = lax.all_gather(mine, 'yl', axis=0)  17.5 us
    all_to_all x2, starting transfers between devices, exchange_sum(): got = lax.all_to_all(parts.astype(BF16), axes, 0, 0).astype(F32)  14.8 us
    all_to_all x1, blocking collectives, gather(): return lax.all_to_all(copies, axes, 0, 0)  11.2 us
    dot_general x8, matrix products, dot(): lax.dot_general(left, right, (((left_dim,), (right_dim,)), ((), ())), pre...  7.77 us
    ppermute x1, starting transfers between devices, per_device(): total = part + lax.ppermute(part.astype(BF16), 'yh', SWAP).astype(F32)  7.23 us
    ppermute x1, waiting for transfers between devices, per_device(): total = part + lax.ppermute(part.astype(BF16), 'yh', SWAP).astype(F32)  5.69 us
  transfers between devices with their start and end apart: 5, of which 5 were waited for; matrix products, arithmetic and copies ran while one was open for 4% of the time, Pallas kernels for 0%

profile of v2, /device:TPU:6, one launch (start us, length us, event | category | flops | bytes accessed | tf_op | source)
XLA Modules:
  0.0 137.5 jit_solution(6726424954079524791)
XLA Ops:
  0.6 0.0 copy-start
  0.6 0.8 maximum_bitcast_fusion
  1.4 33.3 %all-gather.2 = bf16[12,4,2048]{2,1,0:T(4,128)(2,1)S(1)} all-gather(bf16[1,4,2048]{2,1,0:T(4,128)(2,1)S(1)} %maximum_bitcast_fusion), channel_id=2, replica_groups=mesh['yh'=2,'x'=4,'z'=12,'yl'=4,'core'=2] {'z'}, dimensions={0}, use_global_device_ids=true | all-gather | bytes 212992 | tf_op jit(solution)/shard_map/all_gather | solution.py:45
  34.7 17.5 %all-gather.1 = bf16[48,4,2048]{2,1,0:T(4,128)(2,1)S(1)} all-gather(bf16[12,4,2048]{2,1,0:T(4,128)(2,1)S(1)} %all-gather.2), channel_id=3, replica_groups=mesh['yh'=2,'x'=4,'z'=12,'yl'=4,'core'=2] {'yl'}, dimensions={0}, use_global_device_ids=true | all-gather | bytes 983040 | tf_op jit(solution)/shard_map/all_gather | solution.py:46
  52.3 0.2 reshape.15
  52.5 0.0 copy-start.1
  52.5 2.1 %collective-permute-start = (bf16[192,2048]{1,0:T(8,128)(2,1)S(1)}, bf16[192,2048]{1,0:T(8,128)(2,1)S(1)}, u32[]{:S(2)}, u32[]{:S(2)}) collective-permute-start(bf16[192,2048]{1,0:T(8,128)(2,1)S(1)} %reshape.15), channel_id=1, source_target_pairs={{0,1},{1,0},{2,3},{3,2},{4,5},{5,4},{6,7},{7,6},{8,9},{9,8},{10,11... | collective-permute-start | bytes 2359304 | tf_op jit(solution)/shard_map/ppermute | solution.py:48
  54.5 0.1 constant_dynamic-update-slice_fusion.1
  54.6 0.0 copy-start.4
  54.6 2.2 %collective-permute-done = bf16[192,2048]{1,0:T(8,128)(2,1)S(1)} collective-permute-done((bf16[192,2048]{1,0:T(8,128)(2,1)S(1)}, bf16[192,2048]{1,0:T(8,128)(2,1)S(1)}, u32[]{:S(2)}, u32[]{:S(2)}) %collective-permute-start) | collective-permute-done | bytes 786464 | tf_op jit(solution)/shard_map/ppermute | solution.py:48
  56.8 0.1 constant_dynamic-update-slice_fusion
  56.9 0.0 copy-done.1
  56.9 0.0 copy-start.2
  56.9 0.5 fusion.8
  57.4 0.0 copy-done.4
  57.4 0.5 fusion.4
  57.9 0.1 copy-done.2
  58.0 0.0 copy-done
  58.0 0.5 fusion.10
  58.5 1.0 fusion.13
  59.5 4.8 %all-to-all-start = ((bf16[4,3,72,384]{3,2,1,0:T(8,128)(2,1)}), bf16[4,3,72,384]{3,2,1,0:T(8,128)(2,1)S(1)}, u32[]{:S(2)}, u32[]{:S(2)}) async-start(bf16[4,3,72,384]{3,2,1,0:T(8,128)(2,1)} %fusion.13), calls=%async_computation | async-start | bytes 1327104 | tf_op jit(solution)/shard_map/all_to_all | solution.py:31
  64.3 0.1 pad_maximum_fusion
  64.4 9.1 %all-to-all-done = bf16[4,3,72,384]{3,2,1,0:T(8,128)(2,1)S(1)} async-done(((bf16[4,3,72,384]{3,2,1,0:T(8,128)(2,1)}), bf16[4,3,72,384]{3,2,1,0:T(8,128)(2,1)S(1)}, u32[]{:S(2)}, u32[]{:S(2)}) %all-to-all-start) | async-done | bytes 663584 | tf_op jit(solution)/shard_map/all_to_all | solution.py:31
  73.5 0.2 select_reduce_fusion
  73.7 7.2 %collective-permute-start.1 = (bf16[3,72,384]{2,1,0:T(8,128)(2,1)S(1)}, bf16[3,72,384]{2,1,0:T(8,128)(2,1)S(1)}, u32[]{:S(2)}, u32[]{:S(2)}) collective-permute-start(bf16[3,72,384]{2,1,0:T(8,128)(2,1)S(1)} %convert_element_type.44), channel_id=1, source_target_pairs={{0,384},{384,0},{1,385},{385,1},{2,386},{386,2},{3,387},{387,3},{4... | collective-permute-start | bytes 497672 | tf_op jit(solution)/shard_map/ppermute | solution.py:63
  81.0 5.7 %collective-permute-done.1 = bf16[3,72,384]{2,1,0:T(8,128)(2,1)S(1)} collective-permute-done((bf16[3,72,384]{2,1,0:T(8,128)(2,1)S(1)}, bf16[3,72,384]{2,1,0:T(8,128)(2,1)S(1)}, u32[]{:S(2)}, u32[]{:S(2)}) %collective-permute-start.1) | collective-permute-done | bytes 165920 | tf_op jit(solution)/shard_map/ppermute | solution.py:63
  86.7 0.1 multiply_convert_fusion.2
  86.8 0.1 broadcast_in_dim.28
  86.9 11.2 %all_to_all.15 = bf16[4,3,72,384]{3,2,1,0:T(8,128)(2,1)S(1)} all-to-all(bf16[4,3,72,384]{3,2,1,0:T(8,128)(2,1)S(1)} %broadcast_in_dim.28), channel_id=1, replica_groups=mesh['yh'=2,'x'=4,'z'=12,'yl'=4,'core'=2] {'x'}, dimensions={0} | all-to-all | bytes 1327104 | tf_op jit(solution)/shard_map/all_to_all | solution.py:38
  98.1 0.1 fusion.14
  98.2 0.6 fusion.15
  98.8 0.6 convolution_add_fusion
  99.4 0.1 slice.48
  99.5 1.9 %collective-permute-start.2 = (f32[192,1024]{1,0:T(8,128)S(1)}, f32[192,1024]{1,0:T(8,128)S(1)}, u32[]{:S(2)}, u32[]{:S(2)}) collective-permute-start(f32[192,1024]{1,0:T(8,128)S(1)} %slice.48), channel_id=1, source_target_pairs={{0,1},{1,0},{2,3},{3,2},{4,5},{5,4},{6,7},{7,6},{8,9},{9,8},{10,11... | collective-permute-start | bytes 2359304 | tf_op jit(solution)/shard_map/ppermute | solution.py:71
  101.4 2.3 %collective-permute-done.2 = f32[192,1024]{1,0:T(8,128)S(1)} collective-permute-done((f32[192,1024]{1,0:T(8,128)S(1)}, f32[192,1024]{1,0:T(8,128)S(1)}, u32[]{:S(2)}, u32[]{:S(2)}) %collective-permute-start.2) | collective-permute-done | bytes 786464 | tf_op jit(solution)/shard_map/ppermute | solution.py:71
  103.6 0.1 slice_add_fusion
  103.8 0.2 reshape.16
  104.0 0.9 convert_element_type.49
  104.9 10.0 %all-to-all-start.2 = ((bf16[48,4,1024]{2,1,0:T(4,128)(2,1)}), bf16[48,4,1024]{2,1,0:T(4,128)(2,1)S(1)}, u32[]{:S(2)}, u32[]{:S(2)}) async-start(bf16[48,4,1024]{2,1,0:T(4,128)(2,1)} %convert_element_type.49), calls=%async_computation.2 | async-start | bytes 786432 | tf_op jit(solution)/shard_map/all_to_all | solution.py:31
  114.9 0.0 copy-start.3
  114.9 2.5 %fusion.2 = bf16[1024,288]{0,1:T(8,128)(2,1)} fusion(bf16[288,384]{1,0:T(8,128)(2,1)S(1)} %bitcast.43, bf16[384,2048]{1,0:T(8,128)(2,1)} %copy-done.2), kind=kOutput, calls=%fused_computation.8 | convolution fusion | flops 227082240 | bytes 1597440 | tf_op jit(solution)/shard_map/dot_general | solution.py:14
  117.5 0.0 copy-done.3
  117.5 1.3 fusion.1
  118.8 1.3 fusion
  120.1 16.6 %all-to-all-done.2 = bf16[48,4,1024]{2,1,0:T(4,128)(2,1)S(1)} async-done(((bf16[48,4,1024]{2,1,0:T(4,128)(2,1)}), bf16[48,4,1024]{2,1,0:T(4,128)(2,1)S(1)}, u32[]{:S(2)}, u32[]{:S(2)}) %all-to-all-start.2) | async-done | bytes 393248 | tf_op jit(solution)/shard_map/all_to_all | solution.py:31
  136.6 0.9 select_reduce_fusion.1
  (7 shorter events, 0.1 us)
Async XLA Ops:
  0.6 57.4 %copy-start = (bf16[1024,288]{0,1:T(8,128)(2,1)S(1)}, bf16[1024,288]{0,1:T(8,128)(2,1)}, u32[]{:S(2)}) copy-start(bf16[1024,288]{0,1:T(8,128)(2,1)} %param.7) | copy-start | bytes 1769476
  52.5 4.4 %copy-start.1 = (bf16[1024,288]{0,1:T(8,128)(2,1)S(1)}, bf16[1024,288]{0,1:T(8,128)(2,1)}, u32[]{:S(2)}) copy-start(bf16[1024,288]{0,1:T(8,128)(2,1)} %param.8) | copy-start | bytes 1769476
  52.5 4.3 %collective-permute-start = (bf16[192,2048]{1,0:T(8,128)(2,1)S(1)}, bf16[192,2048]{1,0:T(8,128)(2,1)S(1)}, u32[]{:S(2)}, u32[]{:S(2)}) collective-permute-start(bf16[192,2048]{1,0:T(8,128)(2,1)S(1)} %reshape.15), channel_id=1, source_target_pairs={{0,1},{1,0},{2,3},{3,2},{4,5},{5,4},{6,7},{7,6},{8,9},{9,8},{10,11... | collective-permute-start | bytes 2359304 | tf_op jit(solution)/shard_map/ppermute | solution.py:48
  54.6 2.8 %copy-start.4 = (bf16[288,1024]{1,0:T(8,128)(2,1)S(1)}, bf16[288,1024]{1,0:T(8,128)(2,1)}, u32[]{:S(2)}) copy-start(bf16[288,1024]{1,0:T(8,128)(2,1)} %param.9) | copy-start | bytes 1769476
  56.9 1.1 copy-start.2
  59.5 14.0 %all-to-all-start = ((bf16[4,3,72,384]{3,2,1,0:T(8,128)(2,1)}), bf16[4,3,72,384]{3,2,1,0:T(8,128)(2,1)S(1)}, u32[]{:S(2)}, u32[]{:S(2)}) async-start(bf16[4,3,72,384]{3,2,1,0:T(8,128)(2,1)} %fusion.13), calls=%async_computation | async-start | bytes 1327104 | tf_op jit(solution)/shard_map/all_to_all | solution.py:31
  73.7 12.9 %collective-permute-start.1 = (bf16[3,72,384]{2,1,0:T(8,128)(2,1)S(1)}, bf16[3,72,384]{2,1,0:T(8,128)(2,1)S(1)}, u32[]{:S(2)}, u32[]{:S(2)}) collective-permute-start(bf16[3,72,384]{2,1,0:T(8,128)(2,1)S(1)} %convert_element_type.44), channel_id=1, source_target_pairs={{0,384},{384,0},{1,385},{385,1},{2,386},{386,2},{3,387},{387,3},{4... | collective-permute-start | bytes 497672 | tf_op jit(solution)/shard_map/ppermute | solution.py:63
  99.5 4.2 %collective-permute-start.2 = (f32[192,1024]{1,0:T(8,128)S(1)}, f32[192,1024]{1,0:T(8,128)S(1)}, u32[]{:S(2)}, u32[]{:S(2)}) collective-permute-start(f32[192,1024]{1,0:T(8,128)S(1)} %slice.48), channel_id=1, source_target_pairs={{0,1},{1,0},{2,3},{3,2},{4,5},{5,4},{6,7},{7,6},{8,9},{9,8},{10,11... | collective-permute-start | bytes 2359304 | tf_op jit(solution)/shard_map/ppermute | solution.py:71
  104.9 31.7 %all-to-all-start.2 = ((bf16[48,4,1024]{2,1,0:T(4,128)(2,1)}), bf16[48,4,1024]{2,1,0:T(4,128)(2,1)S(1)}, u32[]{:S(2)}, u32[]{:S(2)}) async-start(bf16[48,4,1024]{2,1,0:T(4,128)(2,1)} %convert_element_type.49), calls=%async_computation.2 | async-start | bytes 786432 | tf_op jit(solution)/shard_map/all_to_all | solution.py:31
  114.9 2.6 %copy-start.3 = (bf16[384,2048]{1,0:T(8,128)(2,1)S(1)}, bf16[384,2048]{1,0:T(8,128)(2,1)}, u32[]{:S(2)}) copy-start(bf16[384,2048]{1,0:T(8,128)(2,1)} %copy-done.2) | copy-start | bytes 4718596

commit v3 on v2

--- a/solution.py
+++ b/solution.py
@@ -26,9 +26,11 @@
 
 
 def exchange_sum(parts, axes):
-    me = lax.axis_index(axes)
-    own = lax.dynamic_index_in_dim(parts, me, 0)
-    got = lax.all_to_all(parts.astype(BF16), axes, 0, 0).astype(F32)
+    me, n = lax.axis_index(axes), lax.axis_size(axes)
+    rows = parts.shape[0] // n
+    own = lax.dynamic_slice_in_dim(parts, me * rows, rows, 0)[None]
+    sent = parts.astype(BF16).reshape((n, rows) + parts.shape[1:])
+    got = lax.all_to_all(sent, axes, 0, 0).astype(F32)
     at = lax.broadcasted_iota(jnp.int32, got.shape, 0)
     return jnp.sum(jnp.where(at == me, own, got), axis=0)
 
@@ -42,7 +44,7 @@
     rows, width = tokens.shape
     units = gate_weight.shape[1]
     n_x = lax.axis_size("x")
-    mine = lax.all_gather(jnp.concatenate([tokens, out_grad], 1), "z", axis=0)
+    mine = gather(jnp.concatenate([tokens, out_grad], 1), "z")
     mine = lax.all_gather(mine, "yl", axis=0)
     mine = mine.reshape(-1, 2 * width)
     panel = jnp.concatenate([mine, lax.ppermute(mine, "core", SWAP)])
@@ -59,7 +61,7 @@
         ],
         axis=1,
     )
-    part = exchange_sum(pre, "x")
+    part = exchange_sum(pre, "x")[0]
     total = part + lax.ppermute(part.astype(BF16), "yh", SWAP).astype(F32)
     deltas = gather(jnp.stack(pointwise(total[0], total[1], total[2])), "x")
     hidden = deltas[:, 0].reshape(units, count)
@@ -69,7 +71,9 @@
     partial = dot(gate_delta, gate_weight, 0, 1) + dot(up_delta, up_weight, 0, 1)
     half = count // 2
     acc = partial[:half] + lax.ppermute(partial[half:], "core", SWAP)
-    tokens_grad = exchange_sum(acc.reshape(-1, rows, width), CHIPS).astype(BF16)
+    acc = lax.optimization_barrier(acc.astype(BF16)).reshape(-1, rows, width)
+    acc = lax.all_to_all(acc, CHIPS, 0, 0)
+    tokens_grad = jnp.sum(acc.astype(F32), axis=0).astype(BF16)
 
     down_grad = (dot(hidden, panel_grad, 1, 0) * factor).astype(BF16)
     gate_grad = (dot(panel_in, gate_delta, 0, 1) * factor).astype(BF16)

time: 139 us -> 138 us (level)
  blocking collectives: 62.1 us -> 58.6 us
  starting transfers between devices: 26 us -> 23.2 us
  other arithmetic: 4.16 us -> 5.77 us
    all_gather x1 -> x0, blocking collectives: 33.3 us -> none  [per_device(): mine = lax.all_gather(jnp.concatenate([tokens, out_grad], 1), 'z', axis=0)]
    all_to_all x1 -> x2, blocking collectives: 11.2 us -> 40.1 us  [gather(): return lax.all_to_all(copies, axes, 0, 0)]
    all_to_all x2, starting transfers between devices: 14.8 us -> 12.8 us  [the longest x1 8.08 us: per_device(): acc = lax.all_to_all(acc, CHIPS, 0, 0)]
    convert_element_type x2 -> x1, other arithmetic: 1.87 us -> 0.09 us  [per_device(): acc = lax.optimization_barrier(acc.astype(BF16)).reshape(-1, rows, width)]
    broadcast_in_dim x0 -> x1, other arithmetic: none -> 1.76 us  [exchange_sum(): return jnp.sum(jnp.where(at == me, own, got), axis=0)]
    ppermute x1, waiting for transfers between devices: 5.69 us -> 7.18 us  [per_device(): total = part + lax.ppermute(part.astype(BF16), 'yh', SWAP).astype(F32)]
where the time goes in v3:
time: 138 us; the launch traced here: 136 us
  blocking collectives  58.6 us (42%)
  waiting for transfers between devices  36.9 us (27%)
  starting transfers between devices  23.2 us (17%)
  matrix products  8.85 us (6%)
  other arithmetic  5.77 us (4%)
  local copies, waits for them, and re-layouts  1.45 us (1%)
    all_to_all x2, blocking collectives, gather(): return lax.all_to_all(copies, axes, 0, 0)  40.1 us
    all_gather x1, blocking collectives, per_device(): mine = lax.all_gather(mine, 'yl', axis=0)  18.5 us
    all_to_all x1, waiting for transfers between devices, per_device(): acc = lax.all_to_all(acc, CHIPS, 0, 0)  17.9 us
    dot_general x8, matrix products, dot(): lax.dot_general(left, right, (((left_dim,), (right_dim,)), ((), ())), pre...  8.85 us
    all_to_all x1, starting transfers between devices, per_device(): acc = lax.all_to_all(acc, CHIPS, 0, 0)  8.08 us
    all_to_all x1, waiting for transfers between devices, exchange_sum(): got = lax.all_to_all(sent, axes, 0, 0).astype(F32)  7.44 us
    ppermute x1, waiting for transfers between devices, per_device(): total = part + lax.ppermute(part.astype(BF16), 'yh', SWAP).astype(F32)  7.18 us
    ppermute x1, starting transfers between devices, per_device(): total = part + lax.ppermute(part.astype(BF16), 'yh', SWAP).astype(F32)  6.4 us
  transfers between devices with their start and end apart: 5, of which 5 were waited for; matrix products, arithmetic and copies ran while one was open for 4% of the time, Pallas kernels for 0%

profile of v3, /device:TPU:6, one launch (start us, length us, event | category | flops | bytes accessed | tf_op | source)
XLA Modules:
  0.0 135.6 jit_solution(9502145572758460217)
XLA Ops:
  0.6 0.0 copy-start
  0.6 0.8 pad_maximum_fusion.2
  1.4 0.1 broadcast_in_dim.14
  1.5 28.9 %all_to_all.20 = bf16[12,4,2048]{2,1,0:T(4,128)(2,1)S(1)} all-to-all(bf16[12,4,2048]{2,1,0:T(4,128)(2,1)S(1)} %broadcast_in_dim.14), channel_id=1, replica_groups=mesh['yh'=2,'x'=4,'z'=12,'yl'=4,'core'=2] {'z'}, dimensions={0} | all-to-all | bytes 393216 | tf_op jit(solution)/shard_map/all_to_all | solution.py:40
  30.4 18.5 %all-gather = bf16[48,4,2048]{2,1,0:T(4,128)(2,1)S(1)} all-gather(bf16[12,4,2048]{2,1,0:T(4,128)(2,1)S(1)} %all_to_all.20), channel_id=2, replica_groups=mesh['yh'=2,'x'=4,'z'=12,'yl'=4,'core'=2] {'yl'}, dimensions={0}, use_global_device_ids=true | all-gather | bytes 983040 | tf_op jit(solution)/shard_map/all_gather | solution.py:48
  48.9 0.2 reshape.70
  49.1 0.0 copy-start.1
  49.1 2.1 %collective-permute-start = (bf16[192,2048]{1,0:T(8,128)(2,1)S(1)}, bf16[192,2048]{1,0:T(8,128)(2,1)S(1)}, u32[]{:S(2)}, u32[]{:S(2)}) collective-permute-start(bf16[192,2048]{1,0:T(8,128)(2,1)S(1)} %reshape.70), channel_id=1, source_target_pairs={{0,1},{1,0},{2,3},{3,2},{4,5},{5,4},{6,7},{7,6},{8,9},{9,8},{10,11... | collective-permute-start | bytes 2359304 | tf_op jit(solution)/shard_map/ppermute | solution.py:50
  51.2 0.1 constant_dynamic-update-slice_fusion.1
  51.2 0.0 copy-start.2
  51.2 2.2 %collective-permute-done = bf16[192,2048]{1,0:T(8,128)(2,1)S(1)} collective-permute-done((bf16[192,2048]{1,0:T(8,128)(2,1)S(1)}, bf16[192,2048]{1,0:T(8,128)(2,1)S(1)}, u32[]{:S(2)}, u32[]{:S(2)}) %collective-permute-start) | collective-permute-done | bytes 786464 | tf_op jit(solution)/shard_map/ppermute | solution.py:50
  53.4 0.1 constant_dynamic-update-slice_fusion
  53.5 0.0 copy-done.1
  53.5 1.3 bitcast_convert_fusion.1
  54.8 0.0 copy-done.2
  54.8 1.3 bitcast_convert_fusion
  56.0 0.0 copy-done
  56.0 1.3 bitcast_convert_fusion.2
  57.3 0.9 pad_maximum_fusion
  58.2 4.8 %all-to-all-start.1 = ((bf16[4,1,3,72,384]{4,3,2,1,0:T(8,128)(2,1)}), bf16[4,1,3,72,384]{4,3,2,1,0:T(8,128)(2,1)S(1)}, u32[]{:S(2)}, u32[]{:S(2)}) async-start(bf16[4,1,3,72,384]{4,3,2,1,0:T(8,128)(2,1)} %pad_maximum_fusion), calls=%async_computation.1 | async-start | bytes 1327104 | tf_op jit(solution)/shard_map/all_to_all | solution.py:33
  63.0 1.8 %fusion.15 = f32[3,72,384]{2,1,0:T(8,128)} fusion(s32[]{:T(128)S(6)} %select_n.7, f32[4,1,72,384]{3,2,0,1:T(8,128)} %bitcast.38, f32[4,1,72,384]{3,2,0,1:T(8,128)} %bitcast.36, f32[4,1,72,384]{3,2,0,1:T(8,128)} %bitcast.37), kind=kLoop, calls=%fused_computation.28 | loop fusion | flops 165888 | bytes 1658884 | tf_op jit(solution)/shard_map/jit(_where)/broadcast_in_dim | solution.py:35
  64.8 7.4 %all-to-all-done.1 = bf16[4,1,3,72,384]{4,3,2,1,0:T(8,128)(2,1)S(1)} async-done(((bf16[4,1,3,72,384]{4,3,2,1,0:T(8,128)(2,1)}), bf16[4,1,3,72,384]{4,3,2,1,0:T(8,128)(2,1)S(1)}, u32[]{:S(2)}, u32[]{:S(2)}) %all-to-all-start.1) | async-done | bytes 663584 | tf_op jit(solution)/shard_map/all_to_all | solution.py:33
  72.2 1.2 select_reduce_fusion
  73.5 6.4 %collective-permute-start.1 = (bf16[3,72,384]{2,1,0:T(8,128)(2,1)S(1)}, bf16[3,72,384]{2,1,0:T(8,128)(2,1)S(1)}, u32[]{:S(2)}, u32[]{:S(2)}) collective-permute-start(bf16[3,72,384]{2,1,0:T(8,128)(2,1)S(1)} %convert_element_type.44), channel_id=1, source_target_pairs={{0,384},{384,0},{1,385},{385,1},{2,386},{386,2},{3,387},{387,3},{4... | collective-permute-start | bytes 497672 | tf_op jit(solution)/shard_map/ppermute | solution.py:65
  79.9 7.2 %collective-permute-done.1 = bf16[3,72,384]{2,1,0:T(8,128)(2,1)S(1)} collective-permute-done((bf16[3,72,384]{2,1,0:T(8,128)(2,1)S(1)}, bf16[3,72,384]{2,1,0:T(8,128)(2,1)S(1)}, u32[]{:S(2)}, u32[]{:S(2)}) %collective-permute-start.1) | collective-permute-done | bytes 165920 | tf_op jit(solution)/shard_map/ppermute | solution.py:65
  87.1 0.1 multiply_convert_fusion.2
  87.2 0.1 broadcast_in_dim.26
  87.3 11.2 %all_to_all.21 = bf16[4,3,72,384]{3,2,1,0:T(8,128)(2,1)S(1)} all-to-all(bf16[4,3,72,384]{3,2,1,0:T(8,128)(2,1)S(1)} %broadcast_in_dim.26), channel_id=1, replica_groups=mesh['yh'=2,'x'=4,'z'=12,'yl'=4,'core'=2] {'x'}, dimensions={0} | all-to-all | bytes 1327104 | tf_op jit(solution)/shard_map/all_to_all | solution.py:40
  98.5 0.1 fusion.17
  98.6 0.6 fusion.18
  99.2 0.6 convolution_add_fusion
  99.8 0.1 slice.48
  99.8 1.9 %collective-permute-start.2 = (f32[192,1024]{1,0:T(8,128)S(1)}, f32[192,1024]{1,0:T(8,128)S(1)}, u32[]{:S(2)}, u32[]{:S(2)}) collective-permute-start(f32[192,1024]{1,0:T(8,128)S(1)} %slice.48), channel_id=1, source_target_pairs={{0,1},{1,0},{2,3},{3,2},{4,5},{5,4},{6,7},{7,6},{8,9},{9,8},{10,11... | collective-permute-start | bytes 2359304 | tf_op jit(solution)/shard_map/ppermute | solution.py:73
  101.8 2.3 %collective-permute-done.2 = f32[192,1024]{1,0:T(8,128)S(1)} collective-permute-done((f32[192,1024]{1,0:T(8,128)S(1)}, f32[192,1024]{1,0:T(8,128)S(1)}, u32[]{:S(2)}, u32[]{:S(2)}) %collective-permute-start.2) | collective-permute-done | bytes 786464 | tf_op jit(solution)/shard_map/ppermute | solution.py:73
  104.0 0.1 fusion.3
  104.1 0.9 reshape.71
  105.0 8.1 %all-to-all-start.3 = ((bf16[48,4,1024]{2,1,0:T(4,128)(2,1)}), bf16[48,4,1024]{2,1,0:T(4,128)(2,1)S(1)}, u32[]{:S(2)}, u32[]{:S(2)}) async-start(bf16[48,4,1024]{2,1,0:T(4,128)(2,1)} %reshape.71), calls=%async_computation.3 | async-start | bytes 786432 | tf_op jit(solution)/shard_map/all_to_all | solution.py:75
  113.1 1.3 fusion.2
  114.4 1.3 fusion.1
  115.7 1.3 fusion
  117.0 17.9 %all-to-all-done.3 = bf16[48,4,1024]{2,1,0:T(4,128)(2,1)S(1)} async-done(((bf16[48,4,1024]{2,1,0:T(4,128)(2,1)}), bf16[48,4,1024]{2,1,0:T(4,128)(2,1)S(1)}, u32[]{:S(2)}, u32[]{:S(2)}) %all-to-all-start.3) | async-done | bytes 393248 | tf_op jit(solution)/shard_map/all_to_all | solution.py:75
  134.8 0.8 reduce_sum.22
  (4 shorter events, 0.1 us)
Async XLA Ops:
  0.6 55.4 %copy-start = (bf16[1024,288]{0,1:T(8,128)(2,1)S(1)}, bf16[1024,288]{0,1:T(8,128)(2,1)}, u32[]{:S(2)}) copy-start(bf16[1024,288]{0,1:T(8,128)(2,1)} %param.7) | copy-start | bytes 1769476
  49.1 4.4 %copy-start.1 = (bf16[1024,288]{0,1:T(8,128)(2,1)S(1)}, bf16[1024,288]{0,1:T(8,128)(2,1)}, u32[]{:S(2)}) copy-start(bf16[1024,288]{0,1:T(8,128)(2,1)} %param.8) | copy-start | bytes 1769476
  49.1 4.3 %collective-permute-start = (bf16[192,2048]{1,0:T(8,128)(2,1)S(1)}, bf16[192,2048]{1,0:T(8,128)(2,1)S(1)}, u32[]{:S(2)}, u32[]{:S(2)}) collective-permute-start(bf16[192,2048]{1,0:T(8,128)(2,1)S(1)} %reshape.70), channel_id=1, source_target_pairs={{0,1},{1,0},{2,3},{3,2},{4,5},{5,4},{6,7},{7,6},{8,9},{9,8},{10,11... | collective-permute-start | bytes 2359304 | tf_op jit(solution)/shard_map/ppermute | solution.py:50
  51.2 3.5 %copy-start.2 = (bf16[288,1024]{1,0:T(8,128)(2,1)S(1)}, bf16[288,1024]{1,0:T(8,128)(2,1)}, u32[]{:S(2)}) copy-start(bf16[288,1024]{1,0:T(8,128)(2,1)} %param.9) | copy-start | bytes 1769476
  58.2 14.0 %all-to-all-start.1 = ((bf16[4,1,3,72,384]{4,3,2,1,0:T(8,128)(2,1)}), bf16[4,1,3,72,384]{4,3,2,1,0:T(8,128)(2,1)S(1)}, u32[]{:S(2)}, u32[]{:S(2)}) async-start(bf16[4,1,3,72,384]{4,3,2,1,0:T(8,128)(2,1)} %pad_maximum_fusion), calls=%async_computation.1 | async-start | bytes 1327104 | tf_op jit(solution)/shard_map/all_to_all | solution.py:33
  73.5 13.6 %collective-permute-start.1 = (bf16[3,72,384]{2,1,0:T(8,128)(2,1)S(1)}, bf16[3,72,384]{2,1,0:T(8,128)(2,1)S(1)}, u32[]{:S(2)}, u32[]{:S(2)}) collective-permute-start(bf16[3,72,384]{2,1,0:T(8,128)(2,1)S(1)} %convert_element_type.44), channel_id=1, source_target_pairs={{0,384},{384,0},{1,385},{385,1},{2,386},{386,2},{3,387},{387,3},{4... | collective-permute-start | bytes 497672 | tf_op jit(solution)/shard_map/ppermute | solution.py:65
  99.8 4.2 %collective-permute-start.2 = (f32[192,1024]{1,0:T(8,128)S(1)}, f32[192,1024]{1,0:T(8,128)S(1)}, u32[]{:S(2)}, u32[]{:S(2)}) collective-permute-start(f32[192,1024]{1,0:T(8,128)S(1)} %slice.48), channel_id=1, source_target_pairs={{0,1},{1,0},{2,3},{3,2},{4,5},{5,4},{6,7},{7,6},{8,9},{9,8},{10,11... | collective-permute-start | bytes 2359304 | tf_op jit(solution)/shard_map/ppermute | solution.py:73
  105.0 29.8 %all-to-all-start.3 = ((bf16[48,4,1024]{2,1,0:T(4,128)(2,1)}), bf16[48,4,1024]{2,1,0:T(4,128)(2,1)S(1)}, u32[]{:S(2)}, u32[]{:S(2)}) async-start(bf16[48,4,1024]{2,1,0:T(4,128)(2,1)} %reshape.71), calls=%async_computation.3 | async-start | bytes 786432 | tf_op jit(solution)/shard_map/all_to_all | solution.py:75

commit v4 on v2

--- a/solution.py
+++ b/solution.py
@@ -28,7 +28,8 @@
 def exchange_sum(parts, axes):
     me = lax.axis_index(axes)
     own = lax.dynamic_index_in_dim(parts, me, 0)
-    got = lax.all_to_all(parts.astype(BF16), axes, 0, 0).astype(F32)
+    sent, own = lax.optimization_barrier((parts.astype(BF16), own))
+    got = lax.all_to_all(sent, axes, 0, 0).astype(F32)
     at = lax.broadcasted_iota(jnp.int32, got.shape, 0)
     return jnp.sum(jnp.where(at == me, own, got), axis=0)
 
@@ -42,7 +43,7 @@
     rows, width = tokens.shape
     units = gate_weight.shape[1]
     n_x = lax.axis_size("x")
-    mine = lax.all_gather(jnp.concatenate([tokens, out_grad], 1), "z", axis=0)
+    mine = gather(jnp.concatenate([tokens, out_grad], 1), "z")
     mine = lax.all_gather(mine, "yl", axis=0)
     mine = mine.reshape(-1, 2 * width)
     panel = jnp.concatenate([mine, lax.ppermute(mine, "core", SWAP)])
@@ -68,12 +69,15 @@
 
     partial = dot(gate_delta, gate_weight, 0, 1) + dot(up_delta, up_weight, 0, 1)
     half = count // 2
-    acc = partial[:half] + lax.ppermute(partial[half:], "core", SWAP)
-    tokens_grad = exchange_sum(acc.reshape(-1, rows, width), CHIPS).astype(BF16)
-
+    got = lax.ppermute(partial[half:], "core", SWAP)
+    up_grad = (dot(panel_in, up_delta, 0, 1) * factor).astype(BF16)
+    acc = (partial[:half] + got).astype(BF16)
+    acc, up_grad = lax.optimization_barrier((acc, up_grad))
+    acc = lax.all_to_all(acc.reshape(-1, rows, width), CHIPS, 0, 0)
+    tokens_grad = jnp.sum(acc.astype(F32), axis=0).astype(BF16)
+    tokens_grad, hidden, gate_delta = lax.optimization_barrier((tokens_grad, hidden, gate_delta))
     down_grad = (dot(hidden, panel_grad, 1, 0) * factor).astype(BF16)
     gate_grad = (dot(panel_in, gate_delta, 0, 1) * factor).astype(BF16)
-    up_grad = (dot(panel_in, up_delta, 0, 1) * factor).astype(BF16)
     return tokens_grad, gate_grad, up_grad, down_grad
 
 

time: 139 us -> 137 us (0.986)
  blocking collectives: 62.1 us -> 88.2 us
  waiting for transfers between devices: 35.8 us -> 19.5 us
  starting transfers between devices: 26 us -> 15.2 us
    all_gather x1 -> x0, blocking collectives: 33.3 us -> none  [per_device(): mine = lax.all_gather(jnp.concatenate([tokens, out_grad], 1), 'z', axis=0)]
    all_to_all x0 -> x1, blocking collectives: none -> 29.6 us  [per_device(): acc = lax.all_to_all(acc.reshape(-1, rows, width), CHIPS, 0, 0)]
    all_to_all x1 -> x2, blocking collectives: 11.2 us -> 40.1 us  [gather(): return lax.all_to_all(copies, axes, 0, 0)]
    all_to_all x2 -> x1, waiting for transfers between devices: 25.6 us -> 9.2 us  [exchange_sum(): got = lax.all_to_all(sent, axes, 0, 0).astype(F32)]
    all_to_all x2 -> x1, starting transfers between devices: 14.8 us -> 4.78 us  [exchange_sum(): got = lax.all_to_all(sent, axes, 0, 0).astype(F32)]
    ppermute x1, waiting for transfers between devices: 5.69 us -> 7.18 us  [per_device(): total = part + lax.ppermute(part.astype(BF16), 'yh', SWAP).astype(F32)]
  transfers between devices with their start and end apart: 5 -> 4, of which waited for: 5 -> 4; matrix products, arithmetic and copies ran while one was open for 4% -> 1% of each run, Pallas kernels for 0% -> 0%
where the time goes in v4:
time: 137 us; the launch traced here: 134 us
  blocking collectives  88.2 us (64%)
  waiting for transfers between devices  19.5 us (14%)
  starting transfers between devices  15.2 us (11%)
  matrix products  6.53 us (5%)
  other arithmetic  3.11 us (2%)
    all_to_all x2, blocking collectives, gather(): return lax.all_to_all(copies, axes, 0, 0)  40.1 us
    all_to_all x1, blocking collectives, per_device(): acc = lax.all_to_all(acc.reshape(-1, rows, width), CHIPS, 0, 0)  29.6 us
    all_gather x1, blocking collectives, per_device(): mine = lax.all_gather(mine, 'yl', axis=0)  18.5 us
    all_to_all x1, waiting for transfers between devices, exchange_sum(): got = lax.all_to_all(sent, axes, 0, 0).astype(F32)  9.2 us
    ppermute x1, waiting for transfers between devices, per_device(): total = part + lax.ppermute(part.astype(BF16), 'yh', SWAP).astype(F32)  7.18 us
    dot_general x8, matrix products, dot(): lax.dot_general(left, right, (((left_dim,), (right_dim,)), ((), ())), pre...  6.53 us
    ppermute x1, starting transfers between devices, per_device(): total = part + lax.ppermute(part.astype(BF16), 'yh', SWAP).astype(F32)  6.4 us
    all_to_all x1, starting transfers between devices, exchange_sum(): got = lax.all_to_all(sent, axes, 0, 0).astype(F32)  4.78 us
  transfers between devices with their start and end apart: 4, of which 4 were waited for; matrix products, arithmetic and copies ran while one was open for 1% of the time, Pallas kernels for 0%

profile of v4, /device:TPU:6, one launch (start us, length us, event | category | flops | bytes accessed | tf_op | source)
XLA Modules:
  0.0 134.3 jit_solution(5494292900718976596)
XLA Ops:
  0.6 0.0 copy-start
  0.6 0.8 pad_maximum_fusion.2
  1.4 0.1 broadcast_in_dim.22
  1.5 28.9 %all_to_all.20 = bf16[12,4,2048]{2,1,0:T(4,128)(2,1)S(1)} all-to-all(bf16[12,4,2048]{2,1,0:T(4,128)(2,1)S(1)} %broadcast_in_dim.22), channel_id=1, replica_groups=mesh['yh'=2,'x'=4,'z'=12,'yl'=4,'core'=2] {'z'}, dimensions={0} | all-to-all | bytes 393216 | tf_op jit(solution)/shard_map/all_to_all | solution.py:39
  30.4 18.5 %all-gather = bf16[48,4,2048]{2,1,0:T(4,128)(2,1)S(1)} all-gather(bf16[12,4,2048]{2,1,0:T(4,128)(2,1)S(1)} %all_to_all.20), channel_id=2, replica_groups=mesh['yh'=2,'x'=4,'z'=12,'yl'=4,'core'=2] {'yl'}, dimensions={0}, use_global_device_ids=true | all-gather | bytes 983040 | tf_op jit(solution)/shard_map/all_gather | solution.py:47
  48.9 0.2 reshape.16
  49.1 1.9 %collective-permute-start = (bf16[192,2048]{1,0:T(8,128)(2,1)S(1)}, bf16[192,2048]{1,0:T(8,128)(2,1)S(1)}, u32[]{:S(2)}, u32[]{:S(2)}) collective-permute-start(bf16[192,2048]{1,0:T(8,128)(2,1)S(1)} %reshape.16), channel_id=1, source_target_pairs={{0,1},{1,0},{2,3},{3,2},{4,5},{5,4},{6,7},{7,6},{8,9},{9,8},{10,11... | collective-permute-start | bytes 2359304 | tf_op jit(solution)/shard_map/ppermute | solution.py:49
  51.0 0.0 copy-start.4
  51.0 0.1 constant_dynamic-update-slice_fusion.1
  51.1 0.0 copy-start.1
  51.1 2.2 %collective-permute-done = bf16[192,2048]{1,0:T(8,128)(2,1)S(1)} collective-permute-done((bf16[192,2048]{1,0:T(8,128)(2,1)S(1)}, bf16[192,2048]{1,0:T(8,128)(2,1)S(1)}, u32[]{:S(2)}, u32[]{:S(2)}) %collective-permute-start) | collective-permute-done | bytes 786464 | tf_op jit(solution)/shard_map/ppermute | solution.py:49
  53.3 0.1 constant_dynamic-update-slice_fusion
  53.3 0.0 copy-done.4
  53.3 0.0 copy-start.2
  53.4 0.5 fusion.5
  53.8 0.0 copy-done.1
  53.9 0.5 fusion.9
  54.3 0.1 copy-done.2
  54.5 0.0 copy-done
  54.5 0.5 fusion.11
  55.0 0.9 fusion.14
  55.9 0.1 pad_maximum_fusion
  56.1 4.8 %all-to-all-start.1 = ((bf16[4,3,72,384]{3,2,1,0:T(8,128)(2,1)}), bf16[4,3,72,384]{3,2,1,0:T(8,128)(2,1)S(1)}, u32[]{:S(2)}, u32[]{:S(2)}) async-start(bf16[4,3,72,384]{3,2,1,0:T(8,128)(2,1)} %fusion.14), calls=%async_computation.1 | async-start | bytes 1327104 | tf_op jit(solution)/shard_map/all_to_all | solution.py:32
  60.9 9.2 %all-to-all-done.1 = bf16[4,3,72,384]{3,2,1,0:T(8,128)(2,1)S(1)} async-done(((bf16[4,3,72,384]{3,2,1,0:T(8,128)(2,1)}), bf16[4,3,72,384]{3,2,1,0:T(8,128)(2,1)S(1)}, u32[]{:S(2)}, u32[]{:S(2)}) %all-to-all-start.1) | async-done | bytes 663584 | tf_op jit(solution)/shard_map/all_to_all | solution.py:32
  70.1 0.2 select_reduce_fusion
  70.3 6.4 %collective-permute-start.1 = (bf16[3,72,384]{2,1,0:T(8,128)(2,1)S(1)}, bf16[3,72,384]{2,1,0:T(8,128)(2,1)S(1)}, u32[]{:S(2)}, u32[]{:S(2)}) collective-permute-start(bf16[3,72,384]{2,1,0:T(8,128)(2,1)S(1)} %convert_element_type.40), channel_id=1, source_target_pairs={{0,384},{384,0},{1,385},{385,1},{2,386},{386,2},{3,387},{387,3},{4... | collective-permute-start | bytes 497672 | tf_op jit(solution)/shard_map/ppermute | solution.py:64
  76.7 7.2 %collective-permute-done.1 = bf16[3,72,384]{2,1,0:T(8,128)(2,1)S(1)} collective-permute-done((bf16[3,72,384]{2,1,0:T(8,128)(2,1)S(1)}, bf16[3,72,384]{2,1,0:T(8,128)(2,1)S(1)}, u32[]{:S(2)}, u32[]{:S(2)}) %collective-permute-start.1) | collective-permute-done | bytes 165920 | tf_op jit(solution)/shard_map/ppermute | solution.py:64
  84.0 0.1 multiply_convert_fusion.2
  84.1 0.1 broadcast_in_dim.25
  84.1 11.2 %all_to_all.21 = bf16[4,3,72,384]{3,2,1,0:T(8,128)(2,1)S(1)} all-to-all(bf16[4,3,72,384]{3,2,1,0:T(8,128)(2,1)S(1)} %broadcast_in_dim.25), channel_id=1, replica_groups=mesh['yh'=2,'x'=4,'z'=12,'yl'=4,'core'=2] {'x'}, dimensions={0} | all-to-all | bytes 1327104 | tf_op jit(solution)/shard_map/all_to_all | solution.py:39
  95.4 0.1 fusion.15
  95.4 0.6 fusion.16
  96.0 0.6 convolution_add_fusion
  96.6 0.0 copy-start.3
  96.7 0.1 slice.48
  96.7 2.1 %collective-permute-start.2 = (f32[192,1024]{1,0:T(8,128)S(1)}, f32[192,1024]{1,0:T(8,128)S(1)}, u32[]{:S(2)}, u32[]{:S(2)}) collective-permute-start(f32[192,1024]{1,0:T(8,128)S(1)} %slice.48), channel_id=1, source_target_pairs={{0,1},{1,0},{2,3},{3,2},{4,5},{5,4},{6,7},{7,6},{8,9},{9,8},{10,11... | collective-permute-start | bytes 2359304 | tf_op jit(solution)/shard_map/ppermute | solution.py:72
  98.8 0.0 copy-done.3
  98.8 1.3 fusion.1
  100.1 0.9 collective-permute-done.2
  101.0 0.1 fusion.3
  101.1 0.1 reshape.17
  101.3 29.6 %all_to_all.22 = bf16[48,4,1024]{2,1,0:T(4,128)(2,1)S(1)} all-to-all(bf16[48,4,1024]{2,1,0:T(4,128)(2,1)S(1)} %reshape.17), channel_id=1, replica_groups=mesh['yh'=2,'x'=4,'z'=12,'yl'=4,'core'=2] {'yl','z'}, dimensions={0} | all-to-all | bytes 786432 | tf_op jit(solution)/shard_map/all_to_all | solution.py:76
  130.9 0.8 reduce_sum.22
  131.7 1.3 fusion.2
  133.0 1.3 fusion
  (5 shorter events, 0.1 us)
Async XLA Ops:
  0.6 53.9 %copy-start = (bf16[1024,288]{0,1:T(8,128)(2,1)S(1)}, bf16[1024,288]{0,1:T(8,128)(2,1)}, u32[]{:S(2)}) copy-start(bf16[1024,288]{0,1:T(8,128)(2,1)} %param.7) | copy-start | bytes 1769476
  49.1 4.2 %collective-permute-start = (bf16[192,2048]{1,0:T(8,128)(2,1)S(1)}, bf16[192,2048]{1,0:T(8,128)(2,1)S(1)}, u32[]{:S(2)}, u32[]{:S(2)}) collective-permute-start(bf16[192,2048]{1,0:T(8,128)(2,1)S(1)} %reshape.16), channel_id=1, source_target_pairs={{0,1},{1,0},{2,3},{3,2},{4,5},{5,4},{6,7},{7,6},{8,9},{9,8},{10,11... | collective-permute-start | bytes 2359304 | tf_op jit(solution)/shard_map/ppermute | solution.py:49
  51.0 2.3 %copy-start.4 = (bf16[288,1024]{1,0:T(8,128)(2,1)S(1)}, bf16[288,1024]{1,0:T(8,128)(2,1)}, u32[]{:S(2)}) copy-start(bf16[288,1024]{1,0:T(8,128)(2,1)} %param.9) | copy-start | bytes 1769476
  51.1 2.7 %copy-start.1 = (bf16[1024,288]{0,1:T(8,128)(2,1)S(1)}, bf16[1024,288]{0,1:T(8,128)(2,1)}, u32[]{:S(2)}) copy-start(bf16[1024,288]{0,1:T(8,128)(2,1)} %param.8) | copy-start | bytes 1769476
  53.3 1.2 copy-start.2
  56.1 14.0 %all-to-all-start.1 = ((bf16[4,3,72,384]{3,2,1,0:T(8,128)(2,1)}), bf16[4,3,72,384]{3,2,1,0:T(8,128)(2,1)S(1)}, u32[]{:S(2)}, u32[]{:S(2)}) async-start(bf16[4,3,72,384]{3,2,1,0:T(8,128)(2,1)} %fusion.14), calls=%async_computation.1 | async-start | bytes 1327104 | tf_op jit(solution)/shard_map/all_to_all | solution.py:32
  70.3 13.6 %collective-permute-start.1 = (bf16[3,72,384]{2,1,0:T(8,128)(2,1)S(1)}, bf16[3,72,384]{2,1,0:T(8,128)(2,1)S(1)}, u32[]{:S(2)}, u32[]{:S(2)}) collective-permute-start(bf16[3,72,384]{2,1,0:T(8,128)(2,1)S(1)} %convert_element_type.40), channel_id=1, source_target_pairs={{0,384},{384,0},{1,385},{385,1},{2,386},{386,2},{3,387},{387,3},{4... | collective-permute-start | bytes 497672 | tf_op jit(solution)/shard_map/ppermute | solution.py:64
  96.6 2.1 %copy-start.3 = (bf16[384,2048]{1,0:T(8,128)(2,1)S(1)}, bf16[384,2048]{1,0:T(8,128)(2,1)}, u32[]{:S(2)}) copy-start(bf16[384,2048]{1,0:T(8,128)(2,1)} %copy-done.2) | copy-start | bytes 4718596
  96.7 4.3 %collective-permute-start.2 = (f32[192,1024]{1,0:T(8,128)S(1)}, f32[192,1024]{1,0:T(8,128)S(1)}, u32[]{:S(2)}, u32[]{:S(2)}) collective-permute-start(f32[192,1024]{1,0:T(8,128)S(1)} %slice.48), channel_id=1, source_target_pairs={{0,1},{1,0},{2,3},{3,2},{4,5},{5,4},{6,7},{7,6},{8,9},{9,8},{10,11... | collective-permute-start | bytes 2359304 | tf_op jit(solution)/shard_map/ppermute | solution.py:72

commit v5 on v4

--- a/solution.py
+++ b/solution.py
@@ -28,10 +28,10 @@
 def exchange_sum(parts, axes):
     me = lax.axis_index(axes)
     own = lax.dynamic_index_in_dim(parts, me, 0)
-    sent, own = lax.optimization_barrier((parts.astype(BF16), own))
+    mask = lax.broadcasted_iota(jnp.int32, (parts.shape[0],) + (1,) * (parts.ndim - 1), 0) == me
+    sent, own, mask = lax.optimization_barrier((parts.astype(BF16), own, mask))
     got = lax.all_to_all(sent, axes, 0, 0).astype(F32)
-    at = lax.broadcasted_iota(jnp.int32, got.shape, 0)
-    return jnp.sum(jnp.where(at == me, own, got), axis=0)
+    return jnp.sum(jnp.where(mask, own, got), axis=0)
 
 
 def gather(block, axes):
@@ -75,7 +75,6 @@
     acc, up_grad = lax.optimization_barrier((acc, up_grad))
     acc = lax.all_to_all(acc.reshape(-1, rows, width), CHIPS, 0, 0)
     tokens_grad = jnp.sum(acc.astype(F32), axis=0).astype(BF16)
-    tokens_grad, hidden, gate_delta = lax.optimization_barrier((tokens_grad, hidden, gate_delta))
     down_grad = (dot(hidden, panel_grad, 1, 0) * factor).astype(BF16)
     gate_grad = (dot(panel_in, gate_delta, 0, 1) * factor).astype(BF16)
     return tokens_grad, gate_grad, up_grad, down_grad

time: 137 us -> 133 us (0.971)
  blocking collectives: 88.2 us -> 72.5 us
  waiting for transfers between devices: 19.5 us -> 29.1 us
  starting transfers between devices: 15.2 us -> 18 us
    all_to_all x1, blocking collectives: 29.6 us -> 13.8 us  [exchange_sum(): got = lax.all_to_all(sent, axes, 0, 0).astype(F32)]
    all_to_all x1, waiting for transfers between devices: 9.2 us -> 19.1 us  [per_device(): acc = lax.all_to_all(acc.reshape(-1, rows, width), CHIPS, 0, 0)]
    all_to_all x1, starting transfers between devices: 4.78 us -> 7.73 us  [per_device(): acc = lax.all_to_all(acc.reshape(-1, rows, width), CHIPS, 0, 0)]
  transfers between devices with their start and end apart: 4 -> 4, of which waited for: 4 -> 4; matrix products, arithmetic and copies ran while one was open for 1% -> 3% of each run, Pallas kernels for 0% -> 0%
where the time goes in v5:
time: 133 us; the launch traced here: 131 us
  blocking collectives  72.5 us (55%)
  waiting for transfers between devices  29.1 us (22%)
  starting transfers between devices  18 us (14%)
  matrix products  6.54 us (5%)
  other arithmetic  2.28 us (2%)
  local copies, waits for them, and re-layouts  1.52 us (1%)
    all_to_all x2, blocking collectives, gather(): return lax.all_to_all(copies, axes, 0, 0)  40.2 us
    all_to_all x1, waiting for transfers between devices, per_device(): acc = lax.all_to_all(acc.reshape(-1, rows, width), CHIPS, 0, 0)  19.1 us
    all_gather x1, blocking collectives, per_device(): mine = lax.all_gather(mine, 'yl', axis=0)  18.5 us
    all_to_all x1, blocking collectives, exchange_sum(): got = lax.all_to_all(sent, axes, 0, 0).astype(F32)  13.8 us
    all_to_all x1, starting transfers between devices, per_device(): acc = lax.all_to_all(acc.reshape(-1, rows, width), CHIPS, 0, 0)  7.73 us
    ppermute x1, waiting for transfers between devices, per_device(): total = part + lax.ppermute(part.astype(BF16), 'yh', SWAP).astype(F32)  6.93 us
    dot_general x8, matrix products, dot(): lax.dot_general(left, right, (((left_dim,), (right_dim,)), ((), ())), pre...  6.54 us
    ppermute x1, starting transfers between devices, per_device(): total = part + lax.ppermute(part.astype(BF16), 'yh', SWAP).astype(F32)  6.4 us
  transfers between devices with their start and end apart: 4, of which 4 were waited for; matrix products, arithmetic and copies ran while one was open for 3% of the time, Pallas kernels for 0%

profile of v5, /device:TPU:6, one launch (start us, length us, event | category | flops | bytes accessed | tf_op | source)
XLA Modules:
  0.0 130.8 jit_solution(18293440267165641919)
XLA Ops:
  0.6 0.0 copy-start
  0.6 0.8 pad_maximum_fusion.2
  1.4 0.1 broadcast_in_dim.32
  1.5 28.9 %all_to_all.20 = bf16[12,4,2048]{2,1,0:T(4,128)(2,1)S(1)} all-to-all(bf16[12,4,2048]{2,1,0:T(4,128)(2,1)S(1)} %broadcast_in_dim.32), channel_id=1, replica_groups=mesh['yh'=2,'x'=4,'z'=12,'yl'=4,'core'=2] {'z'}, dimensions={0} | all-to-all | bytes 393216 | tf_op jit(solution)/shard_map/all_to_all | solution.py:39
  30.4 18.5 %all-gather = bf16[48,4,2048]{2,1,0:T(4,128)(2,1)S(1)} all-gather(bf16[12,4,2048]{2,1,0:T(4,128)(2,1)S(1)} %all_to_all.20), channel_id=2, replica_groups=mesh['yh'=2,'x'=4,'z'=12,'yl'=4,'core'=2] {'yl'}, dimensions={0}, use_global_device_ids=true | all-gather | bytes 983040 | tf_op jit(solution)/shard_map/all_gather | solution.py:47
  48.9 0.2 reshape.24
  49.1 1.9 %collective-permute-start = (bf16[192,2048]{1,0:T(8,128)(2,1)S(1)}, bf16[192,2048]{1,0:T(8,128)(2,1)S(1)}, u32[]{:S(2)}, u32[]{:S(2)}) collective-permute-start(bf16[192,2048]{1,0:T(8,128)(2,1)S(1)} %reshape.24), channel_id=1, source_target_pairs={{0,1},{1,0},{2,3},{3,2},{4,5},{5,4},{6,7},{7,6},{8,9},{9,8},{10,11... | collective-permute-start | bytes 2359304 | tf_op jit(solution)/shard_map/ppermute | solution.py:49
  51.0 0.0 copy-start.1
  51.1 0.1 constant_dynamic-update-slice_fusion.1
  51.1 0.0 copy-start.4
  51.1 2.1 %collective-permute-done = bf16[192,2048]{1,0:T(8,128)(2,1)S(1)} collective-permute-done((bf16[192,2048]{1,0:T(8,128)(2,1)S(1)}, bf16[192,2048]{1,0:T(8,128)(2,1)S(1)}, u32[]{:S(2)}, u32[]{:S(2)}) %collective-permute-start) | collective-permute-done | bytes 786464 | tf_op jit(solution)/shard_map/ppermute | solution.py:49
  53.3 0.1 constant_dynamic-update-slice_fusion
  53.3 0.0 copy-done.1
  53.3 0.0 copy-start.2
  53.4 0.5 fusion.9
  53.8 0.0 copy-done.4
  53.9 0.5 fusion.5
  54.3 0.0 copy-done
  54.4 0.5 fusion.11
  54.9 0.1 fusion.14
  55.0 0.1 pad_maximum_fusion
  55.1 13.8 %all_to_all.21 = bf16[4,3,72,384]{3,2,1,0:T(8,128)(2,1)S(1)} all-to-all(bf16[4,3,72,384]{3,2,1,0:T(8,128)(2,1)S(1)} %fusion.14), channel_id=1, replica_groups=mesh['yh'=2,'x'=4,'z'=12,'yl'=4,'core'=2] {'x'}, dimensions={0} | all-to-all | bytes 1327104 | tf_op jit(solution)/shard_map/all_to_all | solution.py:33
  68.9 0.3 select_reduce_fusion
  69.2 6.4 %collective-permute-start.1 = (bf16[3,72,384]{2,1,0:T(8,128)(2,1)S(1)}, bf16[3,72,384]{2,1,0:T(8,128)(2,1)S(1)}, u32[]{:S(2)}, u32[]{:S(2)}) collective-permute-start(bf16[3,72,384]{2,1,0:T(8,128)(2,1)S(1)} %convert_element_type.40), channel_id=1, source_target_pairs={{0,384},{384,0},{1,385},{385,1},{2,386},{386,2},{3,387},{387,3},{4... | collective-permute-start | bytes 497672 | tf_op jit(solution)/shard_map/ppermute | solution.py:64
  75.6 6.9 %collective-permute-done.1 = bf16[3,72,384]{2,1,0:T(8,128)(2,1)S(1)} collective-permute-done((bf16[3,72,384]{2,1,0:T(8,128)(2,1)S(1)}, bf16[3,72,384]{2,1,0:T(8,128)(2,1)S(1)}, u32[]{:S(2)}, u32[]{:S(2)}) %collective-permute-start.1) | collective-permute-done | bytes 165920 | tf_op jit(solution)/shard_map/ppermute | solution.py:64
  82.5 0.1 multiply_convert_fusion.2
  82.6 0.1 broadcast_in_dim.37
  82.7 11.3 %all_to_all.22 = bf16[4,3,72,384]{3,2,1,0:T(8,128)(2,1)S(1)} all-to-all(bf16[4,3,72,384]{3,2,1,0:T(8,128)(2,1)S(1)} %broadcast_in_dim.37), channel_id=1, replica_groups=mesh['yh'=2,'x'=4,'z'=12,'yl'=4,'core'=2] {'x'}, dimensions={0} | all-to-all | bytes 1327104 | tf_op jit(solution)/shard_map/all_to_all | solution.py:39
  94.0 0.1 fusion.15
  94.1 0.6 fusion.16
  94.7 0.6 convolution_add_fusion
  95.3 0.1 slice.48
  95.4 1.9 %collective-permute-start.2 = (f32[192,1024]{1,0:T(8,128)S(1)}, f32[192,1024]{1,0:T(8,128)S(1)}, u32[]{:S(2)}, u32[]{:S(2)}) collective-permute-start(f32[192,1024]{1,0:T(8,128)S(1)} %slice.48), channel_id=1, source_target_pairs={{0,1},{1,0},{2,3},{3,2},{4,5},{5,4},{6,7},{7,6},{8,9},{9,8},{10,11... | collective-permute-start | bytes 2359304 | tf_op jit(solution)/shard_map/ppermute | solution.py:72
  97.3 0.0 copy-done.2
  97.3 1.3 fusion.1
  98.6 0.0 copy-start.3
  98.6 0.9 collective-permute-done.2
  99.5 0.1 fusion.3
  99.6 0.9 reshape.25
  100.5 7.7 %all-to-all-start.3 = ((bf16[48,4,1024]{2,1,0:T(4,128)(2,1)}), bf16[48,4,1024]{2,1,0:T(4,128)(2,1)S(1)}, u32[]{:S(2)}, u32[]{:S(2)}) async-start(bf16[48,4,1024]{2,1,0:T(4,128)(2,1)} %reshape.25), calls=%async_computation.3 | async-start | bytes 786432 | tf_op jit(solution)/shard_map/all_to_all | solution.py:76
  108.3 0.0 copy-done.3
  108.3 1.3 fusion.2
  109.6 1.3 fusion
  110.9 19.1 %all-to-all-done.3 = bf16[48,4,1024]{2,1,0:T(4,128)(2,1)S(1)} async-done(((bf16[48,4,1024]{2,1,0:T(4,128)(2,1)}), bf16[48,4,1024]{2,1,0:T(4,128)(2,1)S(1)}, u32[]{:S(2)}, u32[]{:S(2)}) %all-to-all-start.3) | async-done | bytes 393248 | tf_op jit(solution)/shard_map/all_to_all | solution.py:76
  130.0 0.8 reduce_sum.22
  (5 shorter events, 0.1 us)
Async XLA Ops:
  0.6 53.7 %copy-start = (bf16[1024,288]{0,1:T(8,128)(2,1)S(1)}, bf16[1024,288]{0,1:T(8,128)(2,1)}, u32[]{:S(2)}) copy-start(bf16[1024,288]{0,1:T(8,128)(2,1)} %param.7) | copy-start | bytes 1769476
  49.1 4.2 %collective-permute-start = (bf16[192,2048]{1,0:T(8,128)(2,1)S(1)}, bf16[192,2048]{1,0:T(8,128)(2,1)S(1)}, u32[]{:S(2)}, u32[]{:S(2)}) collective-permute-start(bf16[192,2048]{1,0:T(8,128)(2,1)S(1)} %reshape.24), channel_id=1, source_target_pairs={{0,1},{1,0},{2,3},{3,2},{4,5},{5,4},{6,7},{7,6},{8,9},{9,8},{10,11... | collective-permute-start | bytes 2359304 | tf_op jit(solution)/shard_map/ppermute | solution.py:49
  51.0 2.3 %copy-start.1 = (bf16[1024,288]{0,1:T(8,128)(2,1)S(1)}, bf16[1024,288]{0,1:T(8,128)(2,1)}, u32[]{:S(2)}) copy-start(bf16[1024,288]{0,1:T(8,128)(2,1)} %param.8) | copy-start | bytes 1769476
  51.1 2.7 %copy-start.4 = (bf16[288,1024]{1,0:T(8,128)(2,1)S(1)}, bf16[288,1024]{1,0:T(8,128)(2,1)}, u32[]{:S(2)}) copy-start(bf16[288,1024]{1,0:T(8,128)(2,1)} %param.9) | copy-start | bytes 1769476
  53.3 43.9 %copy-start.2 = (bf16[384,2048]{1,0:T(8,128)(2,1)}, bf16[384,2048]{1,0:T(8,128)(2,1)S(1)}, u32[]{:S(2)}) copy-start(bf16[384,2048]{1,0:T(8,128)(2,1)S(1)} %constant_dynamic-update-slice_fusion) | copy-start | bytes 4718596
  69.2 13.3 %collective-permute-start.1 = (bf16[3,72,384]{2,1,0:T(8,128)(2,1)S(1)}, bf16[3,72,384]{2,1,0:T(8,128)(2,1)S(1)}, u32[]{:S(2)}, u32[]{:S(2)}) collective-permute-start(bf16[3,72,384]{2,1,0:T(8,128)(2,1)S(1)} %convert_element_type.40), channel_id=1, source_target_pairs={{0,384},{384,0},{1,385},{385,1},{2,386},{386,2},{3,387},{387,3},{4... | collective-permute-start | bytes 497672 | tf_op jit(solution)/shard_map/ppermute | solution.py:64
  95.4 4.2 %collective-permute-start.2 = (f32[192,1024]{1,0:T(8,128)S(1)}, f32[192,1024]{1,0:T(8,128)S(1)}, u32[]{:S(2)}, u32[]{:S(2)}) collective-permute-start(f32[192,1024]{1,0:T(8,128)S(1)} %slice.48), channel_id=1, source_target_pairs={{0,1},{1,0},{2,3},{3,2},{4,5},{5,4},{6,7},{7,6},{8,9},{9,8},{10,11... | collective-permute-start | bytes 2359304 | tf_op jit(solution)/shard_map/ppermute | solution.py:72
  98.6 9.7 %copy-start.3 = (bf16[384,2048]{1,0:T(8,128)(2,1)S(1)}, bf16[384,2048]{1,0:T(8,128)(2,1)}, u32[]{:S(2)}) copy-start(bf16[384,2048]{1,0:T(8,128)(2,1)} %copy-done.2) | copy-start | bytes 4718596
  100.5 29.5 %all-to-all-start.3 = ((bf16[48,4,1024]{2,1,0:T(4,128)(2,1)}), bf16[48,4,1024]{2,1,0:T(4,128)(2,1)S(1)}, u32[]{:S(2)}, u32[]{:S(2)}) async-start(bf16[48,4,1024]{2,1,0:T(4,128)(2,1)} %reshape.25), calls=%async_computation.3 | async-start | bytes 786432 | tf_op jit(solution)/shard_map/all_to_all | solution.py:76

commit v6 on v5

--- a/solution.py
+++ b/solution.py
@@ -7,7 +7,7 @@
 F32 = jnp.float32
 BF16 = jnp.bfloat16
 SWAP = [(0, 1), (1, 0)]
-CHIPS = ("yl", "z")
+CHIPS = ("z", "yl")
 
 
 def dot(left, right, left_dim, right_dim):
@@ -43,8 +43,8 @@
     rows, width = tokens.shape
     units = gate_weight.shape[1]
     n_x = lax.axis_size("x")
-    mine = gather(jnp.concatenate([tokens, out_grad], 1), "z")
-    mine = lax.all_gather(mine, "yl", axis=0)
+    mine = gather(jnp.concatenate([tokens, out_grad], 1), "yl")
+    mine = lax.all_gather(mine, "z", axis=0)
     mine = mine.reshape(-1, 2 * width)
     panel = jnp.concatenate([mine, lax.ppermute(mine, "core", SWAP)])
     panel_in, panel_grad = panel[:, :width], panel[:, width:]

time: 133 us -> 132 us (level)
    all_to_all x2, blocking collectives: 40.2 us -> 21.9 us  [gather(): return lax.all_to_all(copies, axes, 0, 0)]
    all_gather x1, blocking collectives: 18.5 us -> 36.5 us  [per_device(): mine = lax.all_gather(mine, 'z', axis=0)]
where the time goes in v6:
time: 132 us; the launch traced here: 130 us
  blocking collectives  72.2 us (55%)
  waiting for transfers between devices  29.7 us (22%)
  starting transfers between devices  16.7 us (13%)
  matrix products  6.54 us (5%)
  other arithmetic  2.28 us (2%)
  local copies, waits for them, and re-layouts  1.48 us (1%)
    all_gather x1, blocking collectives, per_device(): mine = lax.all_gather(mine, 'z', axis=0)  36.5 us
    all_to_all x2, blocking collectives, gather(): return lax.all_to_all(copies, axes, 0, 0)  21.9 us
    all_to_all x1, waiting for transfers between devices, per_device(): acc = lax.all_to_all(acc.reshape(-1, rows, width), CHIPS, 0, 0)  18.9 us
    all_to_all x1, blocking collectives, exchange_sum(): got = lax.all_to_all(sent, axes, 0, 0).astype(F32)  13.8 us
    ppermute x1, waiting for transfers between devices, per_device(): total = part + lax.ppermute(part.astype(BF16), 'yh', SWAP).astype(F32)  7.74 us
    all_to_all x1, starting transfers between devices, per_device(): acc = lax.all_to_all(acc.reshape(-1, rows, width), CHIPS, 0, 0)  7.12 us
    dot_general x8, matrix products, dot(): lax.dot_general(left, right, (((left_dim,), (right_dim,)), ((), ())), pre...  6.54 us
    ppermute x1, starting transfers between devices, per_device(): total = part + lax.ppermute(part.astype(BF16), 'yh', SWAP).astype(F32)  5.71 us
  transfers between devices with their start and end apart: 4, of which 4 were waited for; matrix products, arithmetic and copies ran while one was open for 3% of the time, Pallas kernels for 0%

profile of v6, /device:TPU:6, one launch (start us, length us, event | category | flops | bytes accessed | tf_op | source)
XLA Modules:
  0.0 129.7 jit_solution(5819199042368709417)
XLA Ops:
  0.6 0.0 copy-start
  0.6 0.8 pad_maximum_fusion.2
  1.5 10.4 %all_to_all.20 = bf16[4,4,2048]{2,1,0:T(4,128)(2,1)S(1)} all-to-all(bf16[4,4,2048]{2,1,0:T(4,128)(2,1)S(1)} %broadcast_in_dim.32), channel_id=1, replica_groups=mesh['yh'=2,'x'=4,'z'=12,'yl'=4,'core'=2] {'yl'}, dimensions={0} | all-to-all | bytes 131072 | tf_op jit(solution)/shard_map/all_to_all | solution.py:39
  11.9 36.5 %all-gather = bf16[48,4,2048]{2,1,0:T(4,128)(2,1)S(1)} all-gather(bf16[4,4,2048]{2,1,0:T(4,128)(2,1)S(1)} %all_to_all.20), channel_id=2, replica_groups=mesh['yh'=2,'x'=4,'z'=12,'yl'=4,'core'=2] {'z'}, dimensions={0}, use_global_device_ids=true | all-gather | bytes 851968 | tf_op jit(solution)/shard_map/all_gather | solution.py:47
  48.4 0.2 reshape.24
  48.6 1.9 %collective-permute-start = (bf16[192,2048]{1,0:T(8,128)(2,1)S(1)}, bf16[192,2048]{1,0:T(8,128)(2,1)S(1)}, u32[]{:S(2)}, u32[]{:S(2)}) collective-permute-start(bf16[192,2048]{1,0:T(8,128)(2,1)S(1)} %reshape.24), channel_id=1, source_target_pairs={{0,1},{1,0},{2,3},{3,2},{4,5},{5,4},{6,7},{7,6},{8,9},{9,8},{10,11... | collective-permute-start | bytes 2359304 | tf_op jit(solution)/shard_map/ppermute | solution.py:49
  50.5 0.0 copy-start.1
  50.5 0.1 constant_dynamic-update-slice_fusion.1
  50.6 0.0 copy-start.4
  50.6 2.1 %collective-permute-done = bf16[192,2048]{1,0:T(8,128)(2,1)S(1)} collective-permute-done((bf16[192,2048]{1,0:T(8,128)(2,1)S(1)}, bf16[192,2048]{1,0:T(8,128)(2,1)S(1)}, u32[]{:S(2)}, u32[]{:S(2)}) %collective-permute-start) | collective-permute-done | bytes 786464 | tf_op jit(solution)/shard_map/ppermute | solution.py:49
  52.8 0.1 constant_dynamic-update-slice_fusion
  52.8 0.0 copy-done.1
  52.8 0.0 copy-start.2
  52.8 0.5 fusion.9
  53.3 0.0 copy-done.4
  53.3 0.5 fusion.5
  53.8 0.0 copy-done
  53.8 0.5 fusion.11
  54.3 0.1 fusion.14
  54.5 0.1 pad_maximum_fusion
  54.6 13.8 %all_to_all.21 = bf16[4,3,72,384]{3,2,1,0:T(8,128)(2,1)S(1)} all-to-all(bf16[4,3,72,384]{3,2,1,0:T(8,128)(2,1)S(1)} %fusion.14), channel_id=1, replica_groups=mesh['yh'=2,'x'=4,'z'=12,'yl'=4,'core'=2] {'x'}, dimensions={0} | all-to-all | bytes 1327104 | tf_op jit(solution)/shard_map/all_to_all | solution.py:33
  68.4 0.3 select_reduce_fusion
  68.6 5.7 %collective-permute-start.1 = (bf16[3,72,384]{2,1,0:T(8,128)(2,1)S(1)}, bf16[3,72,384]{2,1,0:T(8,128)(2,1)S(1)}, u32[]{:S(2)}, u32[]{:S(2)}) collective-permute-start(bf16[3,72,384]{2,1,0:T(8,128)(2,1)S(1)} %convert_element_type.40), channel_id=1, source_target_pairs={{0,384},{384,0},{1,385},{385,1},{2,386},{386,2},{3,387},{387,3},{4... | collective-permute-start | bytes 497672 | tf_op jit(solution)/shard_map/ppermute | solution.py:64
  74.4 7.7 %collective-permute-done.1 = bf16[3,72,384]{2,1,0:T(8,128)(2,1)S(1)} collective-permute-done((bf16[3,72,384]{2,1,0:T(8,128)(2,1)S(1)}, bf16[3,72,384]{2,1,0:T(8,128)(2,1)S(1)}, u32[]{:S(2)}, u32[]{:S(2)}) %collective-permute-start.1) | collective-permute-done | bytes 165920 | tf_op jit(solution)/shard_map/ppermute | solution.py:64
  82.1 0.1 multiply_convert_fusion.2
  82.3 0.1 broadcast_in_dim.37
  82.3 11.5 %all_to_all.22 = bf16[4,3,72,384]{3,2,1,0:T(8,128)(2,1)S(1)} all-to-all(bf16[4,3,72,384]{3,2,1,0:T(8,128)(2,1)S(1)} %broadcast_in_dim.37), channel_id=1, replica_groups=mesh['yh'=2,'x'=4,'z'=12,'yl'=4,'core'=2] {'x'}, dimensions={0} | all-to-all | bytes 1327104 | tf_op jit(solution)/shard_map/all_to_all | solution.py:39
  93.8 0.1 fusion.15
  93.9 0.6 fusion.16
  94.5 0.6 convolution_add_fusion
  95.1 0.1 slice.48
  95.2 1.9 %collective-permute-start.2 = (f32[192,1024]{1,0:T(8,128)S(1)}, f32[192,1024]{1,0:T(8,128)S(1)}, u32[]{:S(2)}, u32[]{:S(2)}) collective-permute-start(f32[192,1024]{1,0:T(8,128)S(1)} %slice.48), channel_id=1, source_target_pairs={{0,1},{1,0},{2,3},{3,2},{4,5},{5,4},{6,7},{7,6},{8,9},{9,8},{10,11... | collective-permute-start | bytes 2359304 | tf_op jit(solution)/shard_map/ppermute | solution.py:72
  97.1 0.0 copy-done.2
  97.1 1.3 %fusion.1 = bf16[1024,288]{0,1:T(8,128)(2,1)} fusion(bf16[288,384]{1,0:T(8,128)(2,1)S(1)} %bitcast.40, bf16[384,2048]{1,0:T(8,128)(2,1)S(1)} %constant_dynamic-update-slice_fusion), kind=kOutput, calls=%fused_computation.7 | convolution fusion | flops 227082240 | bytes 1597440 | tf_op jit(solution)/shard_map/dot_general | solution.py:14
  98.4 0.0 copy-start.3
  98.4 0.9 collective-permute-done.2
  99.3 0.1 fusion.3
  99.4 0.9 reshape.25
  100.4 7.1 %all-to-all-start.3 = ((bf16[48,4,1024]{2,1,0:T(4,128)(2,1)}), bf16[48,4,1024]{2,1,0:T(4,128)(2,1)S(1)}, u32[]{:S(2)}, u32[]{:S(2)}) async-start(bf16[48,4,1024]{2,1,0:T(4,128)(2,1)} %reshape.25), calls=%async_computation.3 | async-start | bytes 786432 | tf_op jit(solution)/shard_map/all_to_all | solution.py:76
  107.5 0.0 copy-done.3
  107.5 1.3 %fusion.2 = bf16[1024,288]{0,1:T(8,128)(2,1)} fusion(bf16[288,384]{1,0:T(8,128)(2,1)S(1)} %bitcast.38, bf16[384,2048]{1,0:T(8,128)(2,1)S(1)} %copy-done.3), kind=kOutput, calls=%fused_computation.8 | convolution fusion | flops 227082240 | bytes 1597440 | tf_op jit(solution)/shard_map/dot_general | solution.py:14
  108.8 1.3 fusion
  110.1 18.9 %all-to-all-done.3 = bf16[48,4,1024]{2,1,0:T(4,128)(2,1)S(1)} async-done(((bf16[48,4,1024]{2,1,0:T(4,128)(2,1)}), bf16[48,4,1024]{2,1,0:T(4,128)(2,1)S(1)}, u32[]{:S(2)}, u32[]{:S(2)}) %all-to-all-start.3) | async-done | bytes 393248 | tf_op jit(solution)/shard_map/all_to_all | solution.py:76
  128.9 0.8 reduce_sum.22
  (6 shorter events, 0.2 us)
Async XLA Ops:
  0.6 53.2 %copy-start = (bf16[1024,288]{0,1:T(8,128)(2,1)S(1)}, bf16[1024,288]{0,1:T(8,128)(2,1)}, u32[]{:S(2)}) copy-start(bf16[1024,288]{0,1:T(8,128)(2,1)} %param.7) | copy-start | bytes 1769476
  48.6 4.2 %collective-permute-start = (bf16[192,2048]{1,0:T(8,128)(2,1)S(1)}, bf16[192,2048]{1,0:T(8,128)(2,1)S(1)}, u32[]{:S(2)}, u32[]{:S(2)}) collective-permute-start(bf16[192,2048]{1,0:T(8,128)(2,1)S(1)} %reshape.24), channel_id=1, source_target_pairs={{0,1},{1,0},{2,3},{3,2},{4,5},{5,4},{6,7},{7,6},{8,9},{9,8},{10,11... | collective-permute-start | bytes 2359304 | tf_op jit(solution)/shard_map/ppermute | solution.py:49
  50.5 2.3 %copy-start.1 = (bf16[1024,288]{0,1:T(8,128)(2,1)S(1)}, bf16[1024,288]{0,1:T(8,128)(2,1)}, u32[]{:S(2)}) copy-start(bf16[1024,288]{0,1:T(8,128)(2,1)} %param.8) | copy-start | bytes 1769476
  50.6 2.7 %copy-start.4 = (bf16[288,1024]{1,0:T(8,128)(2,1)S(1)}, bf16[288,1024]{1,0:T(8,128)(2,1)}, u32[]{:S(2)}) copy-start(bf16[288,1024]{1,0:T(8,128)(2,1)} %param.9) | copy-start | bytes 1769476
  52.8 44.3 %copy-start.2 = (bf16[384,2048]{1,0:T(8,128)(2,1)}, bf16[384,2048]{1,0:T(8,128)(2,1)S(1)}, u32[]{:S(2)}) copy-start(bf16[384,2048]{1,0:T(8,128)(2,1)S(1)} %constant_dynamic-update-slice_fusion) | copy-start | bytes 4718596
  68.6 13.5 %collective-permute-start.1 = (bf16[3,72,384]{2,1,0:T(8,128)(2,1)S(1)}, bf16[3,72,384]{2,1,0:T(8,128)(2,1)S(1)}, u32[]{:S(2)}, u32[]{:S(2)}) collective-permute-start(bf16[3,72,384]{2,1,0:T(8,128)(2,1)S(1)} %convert_element_type.40), channel_id=1, source_target_pairs={{0,384},{384,0},{1,385},{385,1},{2,386},{386,2},{3,387},{387,3},{4... | collective-permute-start | bytes 497672 | tf_op jit(solution)/shard_map/ppermute | solution.py:64
  95.2 4.2 %collective-permute-start.2 = (f32[192,1024]{1,0:T(8,128)S(1)}, f32[192,1024]{1,0:T(8,128)S(1)}, u32[]{:S(2)}, u32[]{:S(2)}) collective-permute-start(f32[192,1024]{1,0:T(8,128)S(1)} %slice.48), channel_id=1, source_target_pairs={{0,1},{1,0},{2,3},{3,2},{4,5},{5,4},{6,7},{7,6},{8,9},{9,8},{10,11... | collective-permute-start | bytes 2359304 | tf_op jit(solution)/shard_map/ppermute | solution.py:72
  98.4 9.1 %copy-start.3 = (bf16[384,2048]{1,0:T(8,128)(2,1)S(1)}, bf16[384,2048]{1,0:T(8,128)(2,1)}, u32[]{:S(2)}) copy-start(bf16[384,2048]{1,0:T(8,128)(2,1)} %copy-done.2) | copy-start | bytes 4718596
  100.4 28.6 %all-to-all-start.3 = ((bf16[48,4,1024]{2,1,0:T(4,128)(2,1)}), bf16[48,4,1024]{2,1,0:T(4,128)(2,1)S(1)}, u32[]{:S(2)}, u32[]{:S(2)}) async-start(bf16[48,4,1024]{2,1,0:T(4,128)(2,1)} %reshape.25), calls=%async_computation.3 | async-start | bytes 786432 | tf_op jit(solution)/shard_map/all_to_all | solution.py:76

commit v7 on v6

--- a/solution.py
+++ b/solution.py
@@ -67,14 +67,17 @@
     gate_delta = deltas[:, 1].reshape(units, count)
     up_delta = deltas[:, 2].reshape(units, count)
 
-    partial = dot(gate_delta, gate_weight, 0, 1) + dot(up_delta, up_weight, 0, 1)
     half = count // 2
-    got = lax.ppermute(partial[half:], "core", SWAP)
-    up_grad = (dot(panel_in, up_delta, 0, 1) * factor).astype(BF16)
-    acc = (partial[:half] + got).astype(BF16)
-    acc, up_grad = lax.optimization_barrier((acc, up_grad))
+    give = dot(gate_delta[:, half:], gate_weight, 0, 1) + dot(up_delta[:, half:], up_weight, 0, 1)
+    got = lax.ppermute(give, "core", SWAP)
+    keep = lax.optimization_barrier(
+        dot(gate_delta[:, :half], gate_weight, 0, 1) + dot(up_delta[:, :half], up_weight, 0, 1)
+    )
+    acc = lax.optimization_barrier((keep + got).astype(BF16))
     acc = lax.all_to_all(acc.reshape(-1, rows, width), CHIPS, 0, 0)
     tokens_grad = jnp.sum(acc.astype(F32), axis=0).astype(BF16)
+
+    up_grad = (dot(panel_in, up_delta, 0, 1) * factor).astype(BF16)
     down_grad = (dot(hidden, panel_grad, 1, 0) * factor).astype(BF16)
     gate_grad = (dot(panel_in, gate_delta, 0, 1) * factor).astype(BF16)
     return tokens_grad, gate_grad, up_grad, down_grad

time: 132 us -> 133 us (level)
  local copies, waits for them, and re-layouts: 1.48 us -> 2.95 us
    unnamed x11, local copies, waits for them, and re-layouts: 0.08 us -> 1.63 us
    dot_general x8 -> x10, matrix products: 6.54 us -> 7.05 us  [dot(): lax.dot_general(left, right, (((left_dim,), (right_dim,)), ((), ())), pre...]
  transfers between devices with their start and end apart: 4 -> 4, of which waited for: 4 -> 4; matrix products, arithmetic and copies ran while one was open for 3% -> 4% of each run, Pallas kernels for 0% -> 0%
where the time goes in v7:
time: 133 us; the launch traced here: 131 us
  blocking collectives  72.2 us (54%)
  waiting for transfers between devices  28.9 us (22%)
  starting transfers between devices  16.7 us (13%)
  matrix products  7.05 us (5%)
  local copies, waits for them, and re-layouts  2.95 us (2%)
  other arithmetic  2.28 us (2%)
    all_gather x1, blocking collectives, per_device(): mine = lax.all_gather(mine, 'z', axis=0)  36.5 us
    all_to_all x2, blocking collectives, gather(): return lax.all_to_all(copies, axes, 0, 0)  21.9 us
    all_to_all x1, waiting for transfers between devices, per_device(): acc = lax.all_to_all(acc.reshape(-1, rows, width), CHIPS, 0, 0)  17.6 us
    all_to_all x1, blocking collectives, exchange_sum(): got = lax.all_to_all(sent, axes, 0, 0).astype(F32)  13.8 us
    ppermute x1, waiting for transfers between devices, per_device(): total = part + lax.ppermute(part.astype(BF16), 'yh', SWAP).astype(F32)  7.76 us
    all_to_all x1, starting transfers between devices, per_device(): acc = lax.all_to_all(acc.reshape(-1, rows, width), CHIPS, 0, 0)  7.1 us
    dot_general x10, matrix products, dot(): lax.dot_general(left, right, (((left_dim,), (right_dim,)), ((), ())), pre...  7.05 us
    ppermute x1, starting transfers between devices, per_device(): total = part + lax.ppermute(part.astype(BF16), 'yh', SWAP).astype(F32)  5.71 us
  transfers between devices with their start and end apart: 4, of which 4 were waited for; matrix products, arithmetic and copies ran while one was open for 4% of the time, Pallas kernels for 0%

profile of v7, /device:TPU:6, one launch (start us, length us, event | category | flops | bytes accessed | tf_op | source)
XLA Modules:
  0.0 130.9 jit_solution(5871672030583669179)
XLA Ops:
  0.6 0.0 copy-start
  0.6 0.8 pad_maximum_fusion.2
  1.5 10.4 %all_to_all.20 = bf16[4,4,2048]{2,1,0:T(4,128)(2,1)S(1)} all-to-all(bf16[4,4,2048]{2,1,0:T(4,128)(2,1)S(1)} %broadcast_in_dim.32), channel_id=1, replica_groups=mesh['yh'=2,'x'=4,'z'=12,'yl'=4,'core'=2] {'yl'}, dimensions={0} | all-to-all | bytes 131072 | tf_op jit(solution)/shard_map/all_to_all | solution.py:39
  11.9 36.5 %all-gather = bf16[48,4,2048]{2,1,0:T(4,128)(2,1)S(1)} all-gather(bf16[4,4,2048]{2,1,0:T(4,128)(2,1)S(1)} %all_to_all.20), channel_id=2, replica_groups=mesh['yh'=2,'x'=4,'z'=12,'yl'=4,'core'=2] {'z'}, dimensions={0}, use_global_device_ids=true | all-gather | bytes 851968 | tf_op jit(solution)/shard_map/all_gather | solution.py:47
  48.4 0.2 reshape.24
  48.6 1.9 %collective-permute-start = (bf16[192,2048]{1,0:T(8,128)(2,1)S(1)}, bf16[192,2048]{1,0:T(8,128)(2,1)S(1)}, u32[]{:S(2)}, u32[]{:S(2)}) collective-permute-start(bf16[192,2048]{1,0:T(8,128)(2,1)S(1)} %reshape.24), channel_id=1, source_target_pairs={{0,1},{1,0},{2,3},{3,2},{4,5},{5,4},{6,7},{7,6},{8,9},{9,8},{10,11... | collective-permute-start | bytes 2359304 | tf_op jit(solution)/shard_map/ppermute | solution.py:49
  50.5 0.1 constant_dynamic-update-slice_fusion.1
  50.6 2.2 %collective-permute-done = bf16[192,2048]{1,0:T(8,128)(2,1)S(1)} collective-permute-done((bf16[192,2048]{1,0:T(8,128)(2,1)S(1)}, bf16[192,2048]{1,0:T(8,128)(2,1)S(1)}, u32[]{:S(2)}, u32[]{:S(2)}) %collective-permute-start) | collective-permute-done | bytes 786464 | tf_op jit(solution)/shard_map/ppermute | solution.py:49
  52.8 0.1 constant_dynamic-update-slice_fusion
  52.8 0.0 copy-done
  52.8 0.0 copy-start.2
  52.8 0.0 copy-start.1
  52.9 0.5 fusion.10
  53.3 1.0 copy-done.1
  54.3 0.0 copy-start.4
  54.3 0.5 fusion.8
  54.8 0.0 copy-done.2
  54.8 0.6 copy-done.4
  55.4 0.5 fusion.4
  55.9 0.1 pad_maximum_fusion
  56.0 0.1 fusion.19
  56.1 13.8 %all_to_all.21 = bf16[4,3,72,384]{3,2,1,0:T(8,128)(2,1)S(1)} all-to-all(bf16[4,3,72,384]{3,2,1,0:T(8,128)(2,1)S(1)} %fusion.19), channel_id=1, replica_groups=mesh['yh'=2,'x'=4,'z'=12,'yl'=4,'core'=2] {'x'}, dimensions={0} | all-to-all | bytes 1327104 | tf_op jit(solution)/shard_map/all_to_all | solution.py:33
  69.9 0.3 select_reduce_fusion
  70.2 5.7 %collective-permute-start.1 = (bf16[3,72,384]{2,1,0:T(8,128)(2,1)S(1)}, bf16[3,72,384]{2,1,0:T(8,128)(2,1)S(1)}, u32[]{:S(2)}, u32[]{:S(2)}) collective-permute-start(bf16[3,72,384]{2,1,0:T(8,128)(2,1)S(1)} %convert_element_type.40), channel_id=1, source_target_pairs={{0,384},{384,0},{1,385},{385,1},{2,386},{386,2},{3,387},{387,3},{4... | collective-permute-start | bytes 497672 | tf_op jit(solution)/shard_map/ppermute | solution.py:64
  75.9 7.8 %collective-permute-done.1 = bf16[3,72,384]{2,1,0:T(8,128)(2,1)S(1)} collective-permute-done((bf16[3,72,384]{2,1,0:T(8,128)(2,1)S(1)}, bf16[3,72,384]{2,1,0:T(8,128)(2,1)S(1)}, u32[]{:S(2)}, u32[]{:S(2)}) %collective-permute-start.1) | collective-permute-done | bytes 165920 | tf_op jit(solution)/shard_map/ppermute | solution.py:64
  83.7 0.1 multiply_convert_fusion.2
  83.8 0.1 broadcast_in_dim.37
  83.9 11.5 %all_to_all.22 = bf16[4,3,72,384]{3,2,1,0:T(8,128)(2,1)S(1)} all-to-all(bf16[4,3,72,384]{3,2,1,0:T(8,128)(2,1)S(1)} %broadcast_in_dim.37), channel_id=1, replica_groups=mesh['yh'=2,'x'=4,'z'=12,'yl'=4,'core'=2] {'x'}, dimensions={0} | all-to-all | bytes 1327104 | tf_op jit(solution)/shard_map/all_to_all | solution.py:39
  95.4 0.1 fusion.20
  95.4 0.5 fusion.13
  95.9 0.5 convolution_add_fusion
  96.4 1.9 %collective-permute-start.2 = (f32[192,1024]{1,0:T(8,128)S(1)}, f32[192,1024]{1,0:T(8,128)S(1)}, u32[]{:S(2)}, u32[]{:S(2)}) collective-permute-start(f32[192,1024]{1,0:T(8,128)S(1)} %convolution_add_fusion), channel_id=1, source_target_pairs={{0,1},{1,0},{2,3},{3,2},{4,5},{5,4},{6,7},{7,6},{8,9},{9,8},{10,11... | collective-permute-start | bytes 2359304 | tf_op jit(solution)/shard_map/ppermute | solution.py:72
  98.3 0.4 fusion.16
  98.7 0.4 convolution_add_fusion.1
  99.1 0.0 copy-start.3
  99.1 1.5 %collective-permute-done.2 = f32[192,1024]{1,0:T(8,128)S(1)} collective-permute-done((f32[192,1024]{1,0:T(8,128)S(1)}, f32[192,1024]{1,0:T(8,128)S(1)}, u32[]{:S(2)}, u32[]{:S(2)}) %collective-permute-start.2) | collective-permute-done | bytes 786464 | tf_op jit(solution)/shard_map/ppermute | solution.py:72
  100.6 0.1 add_convert_fusion
  100.7 0.9 reshape.25
  101.6 7.1 %all-to-all-start.3 = ((bf16[48,4,1024]{2,1,0:T(4,128)(2,1)}), bf16[48,4,1024]{2,1,0:T(4,128)(2,1)S(1)}, u32[]{:S(2)}, u32[]{:S(2)}) async-start(bf16[48,4,1024]{2,1,0:T(4,128)(2,1)} %reshape.25), calls=%async_computation.3 | async-start | bytes 786432 | tf_op jit(solution)/shard_map/all_to_all | solution.py:77
  108.7 0.0 copy-done.3
  108.7 1.3 fusion.2
  110.0 1.3 fusion.1
  111.3 1.3 fusion
  112.6 17.6 %all-to-all-done.3 = bf16[48,4,1024]{2,1,0:T(4,128)(2,1)S(1)} async-done(((bf16[48,4,1024]{2,1,0:T(4,128)(2,1)}), bf16[48,4,1024]{2,1,0:T(4,128)(2,1)S(1)}, u32[]{:S(2)}, u32[]{:S(2)}) %all-to-all-start.3) | async-done | bytes 393248 | tf_op jit(solution)/shard_map/all_to_all | solution.py:77
  130.2 0.8 reduce_sum.22
  (6 shorter events, 0.2 us)
Async XLA Ops:
  0.6 52.2 %copy-start = (bf16[1024,288]{0,1:T(8,128)(2,1)S(1)}, bf16[1024,288]{0,1:T(8,128)(2,1)}, u32[]{:S(2)}) copy-start(bf16[1024,288]{0,1:T(8,128)(2,1)} %param.7) | copy-start | bytes 1769476
  48.6 4.2 %collective-permute-start = (bf16[192,2048]{1,0:T(8,128)(2,1)S(1)}, bf16[192,2048]{1,0:T(8,128)(2,1)S(1)}, u32[]{:S(2)}, u32[]{:S(2)}) collective-permute-start(bf16[192,2048]{1,0:T(8,128)(2,1)S(1)} %reshape.24), channel_id=1, source_target_pairs={{0,1},{1,0},{2,3},{3,2},{4,5},{5,4},{6,7},{7,6},{8,9},{9,8},{10,11... | collective-permute-start | bytes 2359304 | tf_op jit(solution)/shard_map/ppermute | solution.py:49
  52.8 2.0 %copy-start.2 = (bf16[384,2048]{1,0:T(8,128)(2,1)}, bf16[384,2048]{1,0:T(8,128)(2,1)S(1)}, u32[]{:S(2)}) copy-start(bf16[384,2048]{1,0:T(8,128)(2,1)S(1)} %constant_dynamic-update-slice_fusion) | copy-start | bytes 4718596
  52.8 1.5 %copy-start.1 = (bf16[1024,288]{0,1:T(8,128)(2,1)S(1)}, bf16[1024,288]{0,1:T(8,128)(2,1)}, u32[]{:S(2)}) copy-start(bf16[1024,288]{0,1:T(8,128)(2,1)} %param.8) | copy-start | bytes 1769476
  54.3 1.1 copy-start.4
  70.2 13.5 %collective-permute-start.1 = (bf16[3,72,384]{2,1,0:T(8,128)(2,1)S(1)}, bf16[3,72,384]{2,1,0:T(8,128)(2,1)S(1)}, u32[]{:S(2)}, u32[]{:S(2)}) collective-permute-start(bf16[3,72,384]{2,1,0:T(8,128)(2,1)S(1)} %convert_element_type.40), channel_id=1, source_target_pairs={{0,384},{384,0},{1,385},{385,1},{2,386},{386,2},{3,387},{387,3},{4... | collective-permute-start | bytes 497672 | tf_op jit(solution)/shard_map/ppermute | solution.py:64
  96.4 4.2 %collective-permute-start.2 = (f32[192,1024]{1,0:T(8,128)S(1)}, f32[192,1024]{1,0:T(8,128)S(1)}, u32[]{:S(2)}, u32[]{:S(2)}) collective-permute-start(f32[192,1024]{1,0:T(8,128)S(1)} %convolution_add_fusion), channel_id=1, source_target_pairs={{0,1},{1,0},{2,3},{3,2},{4,5},{5,4},{6,7},{7,6},{8,9},{9,8},{10,11... | collective-permute-start | bytes 2359304 | tf_op jit(solution)/shard_map/ppermute | solution.py:72
  99.1 9.6 %copy-start.3 = (bf16[384,2048]{1,0:T(8,128)(2,1)S(1)}, bf16[384,2048]{1,0:T(8,128)(2,1)}, u32[]{:S(2)}) copy-start(bf16[384,2048]{1,0:T(8,128)(2,1)} %copy-done.2) | copy-start | bytes 4718596
  101.6 28.6 %all-to-all-start.3 = ((bf16[48,4,1024]{2,1,0:T(4,128)(2,1)}), bf16[48,4,1024]{2,1,0:T(4,128)(2,1)S(1)}, u32[]{:S(2)}, u32[]{:S(2)}) async-start(bf16[48,4,1024]{2,1,0:T(4,128)(2,1)} %reshape.25), calls=%async_computation.3 | async-start | bytes 786432 | tf_op jit(solution)/shard_map/all_to_all | solution.py:77
